TPU v7x, 256 devices: a whole 4x4x8 slice. The times are simulated.
256 devices in a mesh: expert: 32 (over z, y), etp: 8 (over x, core).
Axes of the slice: x: 4, y: 4, z: 8, core: 2. Of those that a mesh axis runs over, the one named last changes fastest.
Arguments:
- tokens: bfloat16 [32768, 2560], P(('expert', 'etp')), may hold values from -6 to 6
- grad_out: bfloat16 [32768, 2560], P(('expert', 'etp')), may hold values from -6 to 6
- router_weight: bfloat16 [2560, 32], replicated, may hold values from -0.125 to 0.125
- expert_choice: int32 [32768, 1], P(('expert', 'etp')), may hold values from 0 to 31; in each aligned block of 128 rows (0 to 127, 128 to 255, ...) at most 6 rows name the same one
- gate_pre: bfloat16 [32, 1536, 4096], P('expert', None, 'etp'), may hold values from -6 to 6
- up_pre: bfloat16 [32, 1536, 4096], P('expert', None, 'etp'), may hold values from -6 to 6
- w_gate: bfloat16 [32, 2560, 4096], P('expert', None, 'etp'), may hold values from -0.125 to 0.125
- w_up: bfloat16 [32, 2560, 4096], P('expert', None, 'etp'), may hold values from -0.125 to 0.125
- w_down: bfloat16 [32, 4096, 2560], P('expert', 'etp'), may hold values from -0.09375 to 0.09375
Outputs:
- token_grad: bfloat16 [32768, 2560], P(('expert', 'etp'))
- router_grad: float32 [2560, 32], replicated
Inputs may be any that keep to these rules, and one draw needn't show every extreme that they name: `expert_choice`: within the 128 tokens of one device no expert is chosen more than 6 times, and in every draw some expert is chosen exactly 6 times by the tokens of some device.
All inputs are finite; a program needn't handle non-finite values.
Results may differ from a plain program's by a relative error of at most 0.015.
Values may be sent and summed in bfloat16 or wider, within the bound.
No kernel may reach another device: no remote copies, remote signals or barrier semaphores. Data moves between devices by JAX's collectives and lax.ppermute only.
A program may use at most 128 MiB of HBM per device.

v0:
```python
import functools

import jax
import jax.numpy as jnp
from jax import lax
from jax.experimental import pallas as pl
from jax.experimental.pallas import tpu as pltpu
from jax.sharding import PartitionSpec as P

CAP = 6
PIECES = 4
GROUPS = 3
TILE = 8
NT = (((1,), (1,)), ((), ()))
TN = (((0,), (0,)), ((), ()))
NN = (((1,), (0,)), ((), ()))
F32 = jnp.float32
BF16 = jnp.bfloat16
PARAMS = pltpu.CompilerParams(vmem_limit_bytes=24 * 2**20)
COLUMNS = 512
HOPS = (0, -1, 1, 2)
COST = pl.CostEstimate(flops=0, transcendentals=0, bytes_accessed=2**20)


def iota(shape, axis):
    return lax.broadcasted_iota(jnp.int32, shape, axis)


def dot(a, b, dims=NN):
    return lax.dot_general(a, b, dims, preferred_element_type=F32)


def target_row(choice, experts):
    count = choice.shape[1]
    picked = (iota((experts, count), 0) == choice).astype(BF16)
    before = (iota((count, count), 0) < iota((count, count), 1)).astype(BF16)
    earlier = dot(picked, before)
    position = jnp.sum(picked.astype(F32) * earlier, axis=0, keepdims=True)
    return choice * CAP + position.astype(jnp.int32)


def hot_rows(target, peers, groups, piece):
    shape = (peers, len(groups) * TILE, target.shape[1])
    row = iota(shape, 1)
    slot = iota(shape, 0) * CAP + groups[0] * 2 + (row >> 3) * 2 + (row & 1)
    hit = (slot == target.reshape(1, 1, -1)) & (((row >> 1) & (PIECES - 1)) == piece)
    return jnp.where(hit, 1.0, 0.0).reshape(-1, target.shape[1]).astype(BF16)


def pack_rows(rows, target, peers, groups):
    width = rows.shape[1] // PIECES
    total = 0.0
    for piece in range(PIECES):
        total = total + dot(hot_rows(target, peers, groups, piece), rows[:, piece * width : (piece + 1) * width])
    return total.astype(BF16)


def pack_kernel(experts, groups, choice_ref, rows_ref, out_ref):
    target = target_row(choice_ref[...], experts)
    out_ref[...] = pack_rows(rows_ref[...], target, experts, groups)


def pack(choice, rows, experts, groups, name):
    width = rows.shape[1] // PIECES
    return pl.pallas_call(
        functools.partial(pack_kernel, experts, groups),
        out_shape=jax.ShapeDtypeStruct((experts * len(groups) * TILE, width), BF16),
        compiler_params=PARAMS,
        cost_estimate=COST,
        name=name,
    )(choice, rows)


def unpack_kernel(groups, packed_ref, *outs):
    width = packed_ref.shape[1]
    take = packed_ref.shape[0] // len(outs)
    rows = outs[0].shape[0]
    target = iota((1, rows), 1)
    for piece in range(PIECES):
        hot = hot_rows(target, rows // CAP, groups, piece)
        for half, out in enumerate(outs):
            part = packed_ref[half * take : (half + 1) * take, :]
            out[:, piece * width : (piece + 1) * width] = dot(hot, part, TN).astype(BF16)


def unpack(packed, groups, slots, halves, name):
    width = packed.shape[1] * PIECES
    return pl.pallas_call(
        functools.partial(unpack_kernel, groups),
        out_shape=[jax.ShapeDtypeStruct((slots // halves, width), BF16)] * halves,
        compiler_params=PARAMS,
        cost_estimate=COST,
        name=name,
    )(packed)


def expert_kernel(first, counts, ids_ref, *refs):
    total = sum(len(c) for c in counts)
    pieces, (gate_ref, up_ref, down_ref, wg_ref, wu_ref) = refs[:total], refs[total : total + 5]
    outs = refs[total + 5 : total + 5 + 2 * len(counts)]
    lhs_ref, out_ref, dg_ref, du_ref, in_sem, out_sem = refs[total + 5 + len(outs) :]
    slots, width = outs[0].shape
    copies, at, number = [], 0, 0
    for chip in counts:
        for rows in chip:
            copies.append(pltpu.make_async_copy(pieces[number], lhs_ref.at[pl.ds(at, rows)], in_sem.at[number]))
            at, number = at + rows, number + 1
    for copy in copies:
        copy.start()
    last, number = [], 0
    for j, chip in enumerate(counts):
        spot = pl.ds(j * 2 * slots, 2 * slots)
        for _ in chip:
            copies[number].wait()
            number += 1
        hidden = dot(lhs_ref[spot, :], down_ref[...], NT)
        own, peer = ids_ref[2 * (first + j)], ids_ref[2 * (first + j) + 1]
        gate = jnp.concatenate([gate_ref[own], gate_ref[peer]], axis=0).astype(F32)
        up = jnp.concatenate([up_ref[own], up_ref[peer]], axis=0).astype(F32)
        sig = jax.nn.sigmoid(gate)
        dg_ref[...] = (hidden * up * sig * (1.0 + gate * (1.0 - sig))).astype(BF16)
        du_ref[...] = (hidden * gate * sig).astype(BF16)

        def tile(at):
            cols = pl.ds(at, COLUMNS)
            terms = dot(dg_ref[...], wg_ref[cols, :], NT) + dot(du_ref[...], wu_ref[cols, :], NT)
            out_ref[spot, cols] = terms.astype(BF16)

        @pl.loop(0, width // COLUMNS)
        def _(i):
            tile(pl.multiple_of(i * COLUMNS, COLUMNS))

        for i in range(2 * j, 2 * j + 2):
            copy = pltpu.make_async_copy(out_ref.at[pl.ds(i * slots, slots)], outs[i], out_sem.at[i])
            copy.start()
            last.append(copy)
    for copy in last:
        copy.wait()


def expert(ids, first, chips, gate, up, down_w, gate_w, up_w, name):
    width = chips[0][0].shape[1]
    slots, hidden = gate.shape[1:]
    blocks = 2 * len(chips)
    counts = tuple(tuple(piece.shape[0] for piece in chip) for chip in chips)
    pieces = [piece for chip in chips for piece in chip]
    vmem = lambda *shape: pltpu.VMEM(shape, BF16)
    anywhere = pl.BlockSpec(memory_space=pl.ANY)
    held = pl.BlockSpec(memory_space=pltpu.VMEM)
    return pl.pallas_call(
        functools.partial(expert_kernel, first, counts),
        in_specs=[pl.BlockSpec(memory_space=pltpu.SMEM)] + [anywhere] * len(pieces) + [held] * 5,
        out_specs=[anywhere] * blocks,
        out_shape=[jax.ShapeDtypeStruct((slots, width), BF16)] * blocks,
        scratch_shapes=[
            vmem(blocks * slots, width), vmem(blocks * slots, width), vmem(2 * slots, hidden), vmem(2 * slots, hidden),
            pltpu.SemaphoreType.DMA((len(pieces),)), pltpu.SemaphoreType.DMA((blocks,)),
        ],
        compiler_params=pltpu.CompilerParams(vmem_limit_bytes=24 * 2**20),
        cost_estimate=pl.CostEstimate(flops=0, transcendentals=0, bytes_accessed=2**20),
        name=name,
    )(ids, *pieces, gate, up, down_w, gate_w, up_w)


def add_kernel(spots, *refs):
    parts, out_ref, held, sem = refs[: len(spots)], refs[len(spots)], refs[len(spots) + 1 : -1], refs[-1]
    copies = []
    for i, (start, part) in enumerate(zip(spots, parts)):
        copies.append(pltpu.make_async_copy(part.at[pl.ds(start, held[i].shape[0])], held[i], sem.at[i]))
    for copy in copies:
        copy.start()
    for copy in copies:
        copy.wait()
    out_ref[...] = sum(ref[...].astype(F32) for ref in held).astype(BF16)


def add(rows, name, *parts):
    width = parts[0][0].shape[1]
    return pl.pallas_call(
        functools.partial(add_kernel, tuple(start for _, start in parts)),
        in_specs=[pl.BlockSpec(memory_space=pl.ANY)] * len(parts),
        out_shape=jax.ShapeDtypeStruct((rows, width), BF16),
        scratch_shapes=[pltpu.VMEM((rows, width), BF16)] * len(parts) + [pltpu.SemaphoreType.DMA((len(parts),))],
        compiler_params=pltpu.CompilerParams(vmem_limit_bytes=12 * 2**20),
        cost_estimate=COST,
        name=name,
    )(*[part for part, _ in parts])


def token_kernel(router_ref, keep_ref, keep_r_ref, *refs):
    parts, toks, (out_ref, column_ref) = refs[:4], refs[4:6], refs[6:]
    router = router_ref[...].astype(F32)
    column = 0.0
    rows = toks[0].shape[0]
    take = out_ref.shape[0] // 2
    for half in range(2):
        spot = slice(half * rows, (half + 1) * rows)
        total = keep_ref[spot, :].astype(F32) + keep_r_ref[spot, :].astype(F32)
        for part in parts[2 * half : 2 * half + 2]:
            total = total + part[...].astype(F32)
        grad = total.astype(BF16).astype(F32)
        tok = toks[half][...].astype(F32)
        score = jax.nn.sigmoid(jnp.sum(tok * router, axis=1, keepdims=True))
        d_logit = jnp.sum(tok * grad, axis=1, keepdims=True) * score * (1.0 - score)
        token_grad = (score * grad + d_logit * router).astype(BF16)
        column = column + jnp.sum(d_logit * tok, axis=0, keepdims=True)
        out_ref[half * take : (half + 1) * take, :] = pack_rows(
            token_grad, iota((1, rows), 1), rows // CAP, tuple(range(GROUPS))
        )
    column_ref[...] = column


def token_math(kept, parts, tok, router, name):
    rows, width = tok[0].shape
    return pl.pallas_call(
        token_kernel,
        out_shape=[
            jax.ShapeDtypeStruct((2 * rows // CAP * GROUPS * TILE, width // PIECES), BF16),
            jax.ShapeDtypeStruct((1, width), F32),
        ],
        compiler_params=PARAMS,
        cost_estimate=COST,
        name=name,
    )(router, *kept, *parts[0], *parts[1], *tok)


def final_kernel(experts, choice_ref, packed_ref, out_ref):
    target = target_row(choice_ref[...], experts)
    width = packed_ref.shape[1]
    for piece in range(PIECES):
        hot = hot_rows(target, experts, tuple(range(GROUPS)), piece)
        out_ref[:, piece * width : (piece + 1) * width] = dot(hot, packed_ref[...], TN).astype(BF16)


def final(choice, packed, experts, name):
    width = packed.shape[1] * PIECES
    return pl.pallas_call(
        functools.partial(final_kernel, experts),
        out_shape=jax.ShapeDtypeStruct((choice.shape[1], width), BF16),
        compiler_params=PARAMS,
        cost_estimate=COST,
        name=name,
    )(choice, packed)


def exchange(x, axis, parts, name):
    shaped = x.reshape(parts, x.shape[0] // parts, x.shape[1])
    with jax.named_scope(name):
        shaped = lax.all_to_all(shaped, axis, split_axis=0, concat_axis=0, tiled=True)
    return shaped.reshape(x.shape)


def after(x, *gates):
    return lax.optimization_barrier((x, *gates))[0]


def local(tokens, grad_out, router_weight, expert_choice, gate_pre, up_pre, w_gate, w_up, w_down):
    width = tokens.shape[1]
    experts = router_weight.shape[1]
    n_expert = lax.axis_size("expert")
    n_etp = lax.axis_size("etp")
    chips = n_etp // 2
    choice = expert_choice.reshape(1, -1)
    hidden = gate_pre.shape[2]
    slots = gate_pre.shape[1] // n_etp
    gate = gate_pre.reshape(n_etp, slots, hidden)
    up = up_pre.reshape(n_etp, slots, hidden)
    weights = (w_down[0], w_gate[0], w_up[0])
    mine = lax.axis_index("etp")
    core = mine % 2
    chip = mine // 2
    router = lax.dynamic_index_in_dim(router_weight.T, lax.axis_index("expert"), 0)
    near = (chip + jnp.array(HOPS, jnp.int32)) % chips * 2
    ids = jnp.stack([near + core, near + 1 - core], axis=1).reshape(-1).astype(jnp.int32)
    choice, ids, router = lax.optimization_barrier((choice, ids, router))

    def shift(x, by, name):
        with jax.named_scope(name):
            return lax.ppermute(x, "etp", [(i, ((i // 2 + by) % chips) * 2 + i % 2) for i in range(n_etp)])

    def swap(x, name):
        with jax.named_scope(name):
            return lax.ppermute(x, "etp", [(i, i ^ 1) for i in range(n_etp)])

    every = tuple(range(GROUPS))
    sent = pack(choice, grad_out, experts, every, "pack_grad")
    arrived = exchange(sent, "expert", n_expert, "grads")
    sent_tok = pack(choice, after(tokens, sent), experts, every, "pack_tok")
    halves = unpack(after(arrived, sent_tok), every, slots, 2, "unpack_grad")

    left = [shift(part, 1, f"left{i}") for i, part in enumerate(halves)]
    right = [shift(halves[i], -1, f"right{i}") for i in (1, 0)][::-1]
    own_x = [swap(part, f"own_x{i}") for i, part in enumerate(halves)]
    packed_tok = exchange(after(sent_tok, own_x[0]), "expert", n_expert, "toks")
    own = [after(halves[0], sent_tok), halves[1]]
    keep, other = expert(ids, 0, [own + own_x], gate, up, *weights, "expert_own")
    keep_r = swap(other, "own_sum")
    left[0], right[1] = after(left[0], keep), after(right[1], keep)
    far = [shift(left[0], 1, "far0"), shift(right[1], -1, "far1")]
    left_x = [swap(part, f"left_x{i}") for i, part in enumerate(left)]
    right_x = [swap(part, f"right_x{i}") for i, part in enumerate(right)]
    lk, lo, rk, ro = expert(ids, 1, [left + left_x, right + right_x], gate, up, *weights, "expert_sides")
    lr, rr = swap(lo, "left_sum"), swap(ro, "right_sum")
    half = slots // 2
    first = add(half, "sum_left0", (lk, 0), (lr, 0)), add(half, "sum_right1", (rk, half), (rr, half))
    far = [after(far[0], lk), after(far[1], lk)]
    far_x = [swap(part, f"far_x{i}") for i, part in enumerate(far)]
    far = [after(far[0], *first), far[1]]
    fk, fo = expert(ids, 3, [far + far_x], gate, up, *weights, "expert_far")
    fr = swap(after(fo, packed_tok), "far_sum")

    to_left = [shift(first[0], -1, "to_left0"), None]
    to_right = [None, shift(first[1], 1, "to_right1")]
    sums = add(half, "sum_far0", (fk, 0), (fr, 0)), add(half, "sum_far1", (fk, half), (fr, half))
    via_right, via_left = shift(sums[0], 1, "via_right"), shift(sums[1], -1, "via_left")
    tok = unpack(after(packed_tok, *sums), every, slots, 2, "unpack_tok")
    gated_r, gated_l, *_ = lax.optimization_barrier((rk, lk, tok[0], to_left[0], to_right[1]))
    to_right[0] = shift(add(half, "sum_right0", (gated_r, 0), (rr, 0), (via_right, 0)), 1, "to_right0")
    to_left[1] = shift(add(half, "sum_left1", (gated_l, half), (lr, half), (via_left, 0)), -1, "to_left1")
    parts = [[to_right[h], to_left[h]] for h in range(2)]
    back, column = token_math([keep, keep_r], parts, tok, router, "token_math")
    returned = exchange(back, "expert", n_expert, "back")
    token_grad = final(choice, returned, experts, "final")

    bit = 1
    while bit < n_etp:
        column = column + lax.ppermute(column, "etp", [(i, i ^ bit) for i in range(n_etp)])
        bit *= 2
    spread = jnp.broadcast_to(after(column, returned).reshape(1, TILE, width // TILE), (n_expert, TILE, width // TILE))
    spread = lax.all_to_all(spread, "expert", split_axis=0, concat_axis=0, tiled=True)
    return (token_grad, spread.reshape(experts, width).T)


def solution(mesh):
    placed = (
        P(("expert", "etp"), None),
        P(("expert", "etp"), None),
        P(),
        P(("expert", "etp"), None),
        P("expert", None, "etp"),
        P("expert", None, "etp"),
        P("expert", None, "etp"),
        P("expert", None, "etp"),
        P("expert", "etp", None),
    )
    return jax.shard_map(
        local,
        mesh=mesh,
        in_specs=placed,
        out_specs=(P(("expert", "etp"), None), P()),
        check_vma=False,
    )
```

profile of v0, /device:TPU:6, one launch (start us, length us, event | category | flops | bytes accessed | tf_op | source)
XLA Modules:
  0.0 211.9 jit_solution(676759314626307694)
XLA Ops:
  1.6 1.1 copy-done.20
  3.4 2.3 %pack_grad.1 = bf16[768,640]{1,0:T(8,128)(2,1)} custom-call(s32[1,128]{1,0:T(1,128)S(1)} %bitcast.36, bf16[128,2560]{1,0:T(8,128)(2,1)S(1)} %copy-done.20), custom_call_target="tpu_custom_call" | custom-call | bytes 1048576 | tf_op jit(solution)/shard_map/pack_grad/pallas_call | solution.py:65
  5.7 11.6 %all-to-all-start = ((bf16[32,24,640]{2,1,0:T(8,128)(2,1)}), bf16[32,24,640]{2,1,0:T(8,128)(2,1)}, u32[]{:S(2)}, u32[]{:S(2)}) async-start(bf16[32,24,640]{2,1,0:T(8,128)(2,1)} %bitcast.4), calls=%async_computation | async-start | bytes 1966080 | tf_op jit(solution)/shard_map/grads/all_to_all | solution.py:249
  17.3 1.3 pack_tok.1
  18.6 1.0 copy-done.7
  19.6 24.5 %all-to-all-done = bf16[32,24,640]{2,1,0:T(8,128)(2,1)} async-done(((bf16[32,24,640]{2,1,0:T(8,128)(2,1)}), bf16[32,24,640]{2,1,0:T(8,128)(2,1)}, u32[]{:S(2)}, u32[]{:S(2)}) %all-to-all-start) | async-done | bytes 983072 | tf_op jit(solution)/shard_map/grads/all_to_all | solution.py:249
  44.2 3.0 %unpack_grad.1 = (bf16[96,2560]{1,0:T(8,128)(2,1)}, bf16[96,2560]{1,0:T(8,128)(2,1)}) custom-call(bf16[768,640]{1,0:T(8,128)(2,1)} %bitcast.5.packed_ref), custom_call_target="tpu_custom_call" | custom-call | bytes 1048576 | tf_op jit(solution)/shard_map/unpack_grad/pallas_call | solution.py:88
  47.7 0.8 collective-permute-start.8
  48.5 2.4 %collective-permute-start.3 = (bf16[96,2560]{1,0:T(8,128)(2,1)}, bf16[96,2560]{1,0:T(8,128)(2,1)}, u32[]{:S(2)}, u32[]{:S(2)}) collective-permute-start(bf16[96,2560]{1,0:T(8,128)(2,1)} %get-tuple-element.39.refs_0_), channel_id=1, source_target_pairs={{0,2},{1,3},{2,4},{3,5},{4,6},{5,7},{6,0},{7,1},{8,10},{9,11},{10,... | collective-permute-start | bytes 1474568 | tf_op jit(solution)/shard_map/left0/ppermute | solution.py:279
  51.0 0.8 copy-done.23
  51.8 3.2 %collective-permute-start.4 = (bf16[96,2560]{1,0:T(8,128)(2,1)}, bf16[96,2560]{1,0:T(8,128)(2,1)}, u32[]{:S(2)}, u32[]{:S(2)}) collective-permute-start(bf16[96,2560]{1,0:T(8,128)(2,1)} %get-tuple-element.40.refs_1_), channel_id=1, source_target_pairs={{0,2},{1,3},{2,4},{3,5},{4,6},{5,7},{6,0},{7,1},{8,10},{9,11},{10,... | collective-permute-start | bytes 1474568 | tf_op jit(solution)/shard_map/left1/ppermute | solution.py:279
  55.0 5.4 %all-to-all-start.1 = ((bf16[32,24,640]{2,1,0:T(8,128)(2,1)}), bf16[32,24,640]{2,1,0:T(8,128)(2,1)}, u32[]{:S(2)}, u32[]{:S(2)}) async-start(bf16[32,24,640]{2,1,0:T(8,128)(2,1)} %bitcast.34), calls=%async_computation.1 | async-start | bytes 1966080 | tf_op jit(solution)/shard_map/toks/all_to_all | solution.py:249
  60.5 1.7 copy-done.2
  62.2 1.7 copy-done.3
  63.9 1.4 copy-done.4
  65.4 1.4 copy-done.6
  66.8 1.0 copy-done.24
  67.8 7.1 %expert_own.1 = (bf16[192,2560]{1,0:T(8,128)(2,1)S(1)}, bf16[192,2560]{1,0:T(8,128)(2,1)S(1)}) custom-call(s32[8]{0:T(128)S(1)} %reshape.41.ids_ref, bf16[96,2560]{1,0:T(8,128)(2,1)} %get-tuple-element.39.refs_0_, bf16[96,2560]{1,0:T(8,128)(2,1)} %get-tuple-element.40.refs_1_, bf16[96,2560]{1,0:T(8,128)(2,1)S(1)} %copy-done.24, ...), custom_call_target="tpu_custom_call" | custom-call | bytes 1048576 | tf_op jit(solution)/shard_map/expert_own/pallas_call | solution.py:150
  74.9 1.0 copy-done.18
  75.8 1.0 copy-done.27
  77.9 2.4 %collective-permute-done.9.refs_6_ = bf16[96,2560]{1,0:T(8,128)(2,1)S(1)} collective-permute-done((bf16[96,2560]{1,0:T(8,128)(2,1)}, bf16[96,2560]{1,0:T(8,128)(2,1)S(1)}, u32[]{:S(2)}, u32[]{:S(2)}) %collective-permute-start.9) | collective-permute-done | bytes 491552 | tf_op jit(solution)/shard_map/right_x0/ppermute | solution.py:283
  81.0 12.4 %expert_sides.1 = (bf16[192,2560]{1,0:T(8,128)(2,1)S(1)}, bf16[192,2560]{1,0:T(8,128)(2,1)S(1)}, bf16[192,2560]{1,0:T(8,128)(2,1)S(1)}, bf16[192,2560]{1,0:T(8,128)(2,1)S(1)}) custom-call(s32[8]{0:T(128)S(1)} %reshape.41.ids_ref, bf16[96,2560]{1,0:T(8,128)(2,1)} %collective-permute-done.3.refs_0_, bf16[96,2560]{1,0:T(8,128)(2,1)} %collective-permute-done.4.refs_1_, ...), custom_call_target="tpu_custom_call" | custom-call | bytes 1048576 | tf_op jit(solution)/shard_map/expert_sides/pallas_call | solution.py:150
  97.0 0.9 copy-done.8
  99.8 6.9 %expert_far.1 = (bf16[192,2560]{1,0:T(8,128)(2,1)S(1)}, bf16[192,2560]{1,0:T(8,128)(2,1)S(1)}) custom-call(s32[8]{0:T(128)S(1)} %reshape.41.ids_ref, bf16[96,2560]{1,0:T(8,128)(2,1)S(1)} %collective-permute-done.11.refs_0_, bf16[96,2560]{1,0:T(8,128)(2,1)S(1)} %collective-permute-done.14.refs_1_, bf16[96,2560]{1,0:T(8,128)(2,1)S(1)} %collective-permute-done.15.refs_2_, ...), custom_call_target="tpu_custom_call" | custom-call | bytes 1048576 | tf_op jit(solution)/shard_map/expert_far/pallas_call | solution.py:150
  106.7 1.0 copy-done.16
  107.7 1.0 copy-done.28
  108.8 3.2 %collective-permute-start.19 = (bf16[96,2560]{1,0:T(8,128)(2,1)}, bf16[96,2560]{1,0:T(8,128)(2,1)S(1)}, u32[]{:S(2)}, u32[]{:S(2)}) collective-permute-start(bf16[96,2560]{1,0:T(8,128)(2,1)} %copy-done.22), channel_id=1, source_target_pairs={{0,2},{1,3},{2,4},{3,5},{4,6},{5,7},{6,0},{7,1},{8,10},{9,11},{10,... | collective-permute-start | bytes 1474568 | tf_op jit(solution)/shard_map/to_right1/ppermute | solution.py:279
  112.1 1.2 copy-done.17
  114.1 2.0 collective-permute-start.20
  117.2 2.1 %unpack_tok.1 = (bf16[96,2560]{1,0:T(8,128)(2,1)S(1)}, bf16[96,2560]{1,0:T(8,128)(2,1)S(1)}) custom-call(bf16[768,640]{1,0:T(8,128)(2,1)} %bitcast.12.packed_ref), custom_call_target="tpu_custom_call" | custom-call | bytes 1048576 | tf_op jit(solution)/shard_map/unpack_tok/pallas_call | solution.py:88
  119.4 4.7 %collective-permute-done.18.refs_1_ = bf16[96,2560]{1,0:T(8,128)(2,1)S(1)} collective-permute-done((bf16[96,2560]{1,0:T(8,128)(2,1)S(1)}, bf16[96,2560]{1,0:T(8,128)(2,1)S(1)}, u32[]{:S(2)}, u32[]{:S(2)}) %collective-permute-start.18) | collective-permute-done | bytes 491552 | tf_op jit(solution)/shard_map/to_left0/ppermute | solution.py:279
  124.1 9.4 %collective-permute-done.20.refs_2_ = bf16[96,2560]{1,0:T(8,128)(2,1)S(1)} collective-permute-done((bf16[96,2560]{1,0:T(8,128)(2,1)S(1)}, bf16[96,2560]{1,0:T(8,128)(2,1)S(1)}, u32[]{:S(2)}, u32[]{:S(2)}) %collective-permute-start.20) | collective-permute-done | bytes 491552 | tf_op jit(solution)/shard_map/via_right/ppermute | solution.py:279
  133.6 1.1 sum_right0.1
  134.7 3.8 %collective-permute-start.21 = (bf16[96,2560]{1,0:T(8,128)(2,1)S(1)}, bf16[96,2560]{1,0:T(8,128)(2,1)S(1)}, u32[]{:S(2)}, u32[]{:S(2)}) collective-permute-start(bf16[96,2560]{1,0:T(8,128)(2,1)S(1)} %sum_right0.1), channel_id=1, source_target_pairs={{0,2},{1,3},{2,4},{3,5},{4,6},{5,7},{6,0},{7,1},{8,10},{9,11},{10,... | collective-permute-start | bytes 1474568 | tf_op jit(solution)/shard_map/to_right0/ppermute | solution.py:279
  138.5 1.1 sum_left1.1
  139.7 8.6 %collective-permute-done.21.refs_0_ = bf16[96,2560]{1,0:T(8,128)(2,1)S(1)} collective-permute-done((bf16[96,2560]{1,0:T(8,128)(2,1)S(1)}, bf16[96,2560]{1,0:T(8,128)(2,1)S(1)}, u32[]{:S(2)}, u32[]{:S(2)}) %collective-permute-start.21) | collective-permute-done | bytes 491552 | tf_op jit(solution)/shard_map/to_right0/ppermute | solution.py:279
  148.4 4.7 %collective-permute-done.23.refs_3_ = bf16[96,2560]{1,0:T(8,128)(2,1)S(1)} collective-permute-done((bf16[96,2560]{1,0:T(8,128)(2,1)S(1)}, bf16[96,2560]{1,0:T(8,128)(2,1)S(1)}, u32[]{:S(2)}, u32[]{:S(2)}) %collective-permute-start.23) | collective-permute-done | bytes 491552 | tf_op jit(solution)/shard_map/to_left1/ppermute | solution.py:279
  153.0 3.4 %token_math.1 = (bf16[768,640]{1,0:T(8,128)(2,1)}, f32[1,2560]{1,0:T(1,128)S(1)}) custom-call(bf16[1,2560]{1,0:T(2,128)(2,1)S(1)} %dynamic-slice_bitcast_fusion.router_ref, bf16[192,2560]{1,0:T(8,128)(2,1)S(1)} %copy-done.19, bf16[192,2560]{1,0:T(8,128)(2,1)S(1)} %collective-permute-done.2.keep_r_ref, bf16[96,2560]{1,0:T(8,128)(2,1)S(1)} %collective-permute-done.21.refs_0_, ...), custom_call_target="tpu_custom_call" | custom-call | bytes 1048576 | tf_op jit(solution)/shard_map/token_math/pallas_call | solution.py:215
  156.4 9.7 %all-to-all-start.2 = ((bf16[32,24,640]{2,1,0:T(8,128)(2,1)}), bf16[32,24,640]{2,1,0:T(8,128)(2,1)S(1)}, u32[]{:S(2)}, u32[]{:S(2)}) async-start(bf16[32,24,640]{2,1,0:T(8,128)(2,1)} %bitcast.13), calls=%async_computation.2 | async-start | bytes 1966080 | tf_op jit(solution)/shard_map/back/all_to_all | solution.py:249
  166.2 1.2 collective-permute-done.24
  167.5 3.7 %collective-permute-done.25 = f32[1,2560]{1,0:T(1,128)S(1)} collective-permute-done((f32[1,2560]{1,0:T(1,128)S(1)}, f32[1,2560]{1,0:T(1,128)S(1)}, u32[]{:S(2)}, u32[]{:S(2)}) %collective-permute-start.25) | collective-permute-done | bytes 10272 | tf_op jit(solution)/shard_map/ppermute | solution.py:327
  171.2 5.2 %collective-permute-done.26 = f32[1,2560]{1,0:T(1,128)S(1)} collective-permute-done((f32[1,2560]{1,0:T(1,128)S(1)}, f32[1,2560]{1,0:T(1,128)S(1)}, u32[]{:S(2)}, u32[]{:S(2)}) %collective-permute-start.26) | collective-permute-done | bytes 10272 | tf_op jit(solution)/shard_map/ppermute | solution.py:327
  176.4 15.1 %all-to-all-done.2 = bf16[32,24,640]{2,1,0:T(8,128)(2,1)S(1)} async-done(((bf16[32,24,640]{2,1,0:T(8,128)(2,1)}), bf16[32,24,640]{2,1,0:T(8,128)(2,1)S(1)}, u32[]{:S(2)}, u32[]{:S(2)}) %all-to-all-start.2) | async-done | bytes 983072 | tf_op jit(solution)/shard_map/back/all_to_all | solution.py:249
  191.7 0.8 broadcast_in_dim.8
  192.5 5.0 %all-to-all-start.3 = ((f32[32,8,320]{2,1,0:T(8,128)}), f32[32,8,320]{2,1,0:T(8,128)S(1)}, u32[]{:S(2)}, u32[]{:S(2)}) async-start(f32[32,8,320]{2,1,0:T(8,128)} %broadcast_in_dim.8), calls=%async_computation.3 | async-start | bytes 786432 | tf_op jit(solution)/shard_map/all_to_all | solution.py:330
  197.4 1.8 final.1
  199.2 11.8 %all-to-all-done.3 = f32[32,8,320]{2,1,0:T(8,128)S(1)} async-done(((f32[32,8,320]{2,1,0:T(8,128)}), f32[32,8,320]{2,1,0:T(8,128)S(1)}, u32[]{:S(2)}, u32[]{:S(2)}) %all-to-all-start.3) | async-done | bytes 327712 | tf_op jit(solution)/shard_map/all_to_all | solution.py:330
  211.1 0.8 reshape.50
  (100 shorter events, 11.9 us)
Async XLA Ops:
  0.6 16.6 %copy-start.26 = (s32[128,1]{0,1:T(1,128)S(1)}, s32[128,1]{0,1:T(1,128)}, u32[]{:S(2)}) copy-start(s32[128,1]{0,1:T(1,128)} %param.13) | copy-start | bytes 1540
  1.6 1.1 copy-start.20
  3.4 13.9 %copy-start.21 = (bf16[128,2560]{1,0:T(8,128)(2,1)S(1)}, bf16[128,2560]{1,0:T(8,128)(2,1)}, u32[]{:S(2)}) copy-start(bf16[128,2560]{1,0:T(8,128)(2,1)} %rows_ref.2) | copy-start | bytes 1966084
  5.7 38.5 %all-to-all-start = ((bf16[32,24,640]{2,1,0:T(8,128)(2,1)}), bf16[32,24,640]{2,1,0:T(8,128)(2,1)}, u32[]{:S(2)}, u32[]{:S(2)}) async-start(bf16[32,24,640]{2,1,0:T(8,128)(2,1)} %bitcast.4), calls=%async_computation | async-start | bytes 1966080 | tf_op jit(solution)/shard_map/grads/all_to_all | solution.py:249
  17.3 43.2 %copy-start.1 = (bf16[1,512,2560]{2,1,0:T(8,128)(2,1)S(1)}, bf16[1,512,2560]{2,1,0:T(8,128)(2,1)}, u32[]{:S(2)}) copy-start(bf16[1,512,2560]{2,1,0:T(8,128)(2,1)} %param.18) | copy-start | bytes 7864324
  47.2 3.8 %collective-permute-start = (bf16[96,2560]{1,0:T(8,128)(2,1)}, bf16[96,2560]{1,0:T(8,128)(2,1)S(1)}, u32[]{:S(2)}, u32[]{:S(2)}) collective-permute-start(bf16[96,2560]{1,0:T(8,128)(2,1)} %get-tuple-element.39.refs_0_), channel_id=1, source_target_pairs={{0,1},{1,0},{2,3},{3,2},{4,5},{5,4},{6,7},{7,6},{8,9},{9,8},{10,11... | collective-permute-start | bytes 1474568 | tf_op jit(solution)/shard_map/own_x0/ppermute | solution.py:283
  47.2 13.2 %collective-permute-start.1 = (bf16[96,2560]{1,0:T(8,128)(2,1)}, bf16[96,2560]{1,0:T(8,128)(2,1)}, u32[]{:S(2)}, u32[]{:S(2)}) collective-permute-start(bf16[96,2560]{1,0:T(8,128)(2,1)} %get-tuple-element.40.refs_1_), channel_id=1, source_target_pairs={{0,1},{1,0},{2,3},{3,2},{4,5},{5,4},{6,7},{7,6},{8,9},{9,8},{10,11... | collective-permute-start | bytes 1474568 | tf_op jit(solution)/shard_map/own_x1/ppermute | solution.py:283
  47.7 29.1 %collective-permute-start.8 = (bf16[96,2560]{1,0:T(8,128)(2,1)}, bf16[96,2560]{1,0:T(8,128)(2,1)S(1)}, u32[]{:S(2)}, u32[]{:S(2)}) collective-permute-start(bf16[96,2560]{1,0:T(8,128)(2,1)} %get-tuple-element.40.refs_1_), channel_id=1, source_target_pairs={{0,6},{1,7},{2,0},{3,1},{4,2},{5,3},{6,4},{7,5},{8,14},{9,15},{10,... | collective-permute-start | bytes 1474568 | tf_op jit(solution)/shard_map/right1/ppermute | solution.py:279
  48.5 28.3 %collective-permute-start.3 = (bf16[96,2560]{1,0:T(8,128)(2,1)}, bf16[96,2560]{1,0:T(8,128)(2,1)}, u32[]{:S(2)}, u32[]{:S(2)}) collective-permute-start(bf16[96,2560]{1,0:T(8,128)(2,1)} %get-tuple-element.39.refs_0_), channel_id=1, source_target_pairs={{0,2},{1,3},{2,4},{3,5},{4,6},{5,7},{6,0},{7,1},{8,10},{9,11},{10,... | collective-permute-start | bytes 1474568 | tf_op jit(solution)/shard_map/left0/ppermute | solution.py:279
  51.0 25.9 %collective-permute-start.7 = (bf16[96,2560]{1,0:T(8,128)(2,1)}, bf16[96,2560]{1,0:T(8,128)(2,1)}, u32[]{:S(2)}, u32[]{:S(2)}) collective-permute-start(bf16[96,2560]{1,0:T(8,128)(2,1)} %get-tuple-element.39.refs_0_), channel_id=1, source_target_pairs={{0,6},{1,7},{2,0},{3,1},{4,2},{5,3},{6,4},{7,5},{8,14},{9,15},{10,... | collective-permute-start | bytes 1474568 | tf_op jit(solution)/shard_map/right0/ppermute | solution.py:279
  51.8 25.6 %collective-permute-start.4 = (bf16[96,2560]{1,0:T(8,128)(2,1)}, bf16[96,2560]{1,0:T(8,128)(2,1)}, u32[]{:S(2)}, u32[]{:S(2)}) collective-permute-start(bf16[96,2560]{1,0:T(8,128)(2,1)} %get-tuple-element.40.refs_1_), channel_id=1, source_target_pairs={{0,2},{1,3},{2,4},{3,5},{4,6},{5,7},{6,0},{7,1},{8,10},{9,11},{10,... | collective-permute-start | bytes 1474568 | tf_op jit(solution)/shard_map/left1/ppermute | solution.py:279
  55.0 53.7 %all-to-all-start.1 = ((bf16[32,24,640]{2,1,0:T(8,128)(2,1)}), bf16[32,24,640]{2,1,0:T(8,128)(2,1)}, u32[]{:S(2)}, u32[]{:S(2)}) async-start(bf16[32,24,640]{2,1,0:T(8,128)(2,1)} %bitcast.34), calls=%async_computation.1 | async-start | bytes 1966080 | tf_op jit(solution)/shard_map/toks/all_to_all | solution.py:249
  60.5 1.7 copy-start.2
  62.2 1.7 copy-start.3
  63.9 1.4 copy-start.4
  65.3 1.4 copy-start.6
  67.8 13.2 %copy-start.5 = (bf16[1,1536,512]{2,1,0:T(8,128)(2,1)S(1)}, bf16[1,1536,512]{2,1,0:T(8,128)(2,1)}, u32[]{:S(2)}) copy-start(bf16[1,1536,512]{2,1,0:T(8,128)(2,1)} %param.14) | copy-start | bytes 4718596
  76.8 4.2 %collective-permute-start.5 = (bf16[96,2560]{1,0:T(8,128)(2,1)}, bf16[96,2560]{1,0:T(8,128)(2,1)S(1)}, u32[]{:S(2)}, u32[]{:S(2)}) collective-permute-start(bf16[96,2560]{1,0:T(8,128)(2,1)} %collective-permute-done.3.refs_0_), channel_id=1, source_target_pairs={{0,1},{1,0},{2,3},{3,2},{4,5},{5,4},{6,7},{7,6},{8,9},{9,8},{10,11... | collective-permute-start | bytes 1474568 | tf_op jit(solution)/shard_map/left_x0/ppermute | solution.py:283
  76.8 3.5 %collective-permute-start.9 = (bf16[96,2560]{1,0:T(8,128)(2,1)}, bf16[96,2560]{1,0:T(8,128)(2,1)S(1)}, u32[]{:S(2)}, u32[]{:S(2)}) collective-permute-start(bf16[96,2560]{1,0:T(8,128)(2,1)} %collective-permute-done.7.refs_4_), channel_id=1, source_target_pairs={{0,1},{1,0},{2,3},{3,2},{4,5},{5,4},{6,7},{7,6},{8,9},{9,8},{10,11... | collective-permute-start | bytes 1474568 | tf_op jit(solution)/shard_map/right_x0/ppermute | solution.py:283
  77.3 3.7 %collective-permute-start.6 = (bf16[96,2560]{1,0:T(8,128)(2,1)}, bf16[96,2560]{1,0:T(8,128)(2,1)S(1)}, u32[]{:S(2)}, u32[]{:S(2)}) collective-permute-start(bf16[96,2560]{1,0:T(8,128)(2,1)} %collective-permute-done.4.refs_1_), channel_id=1, source_target_pairs={{0,1},{1,0},{2,3},{3,2},{4,5},{5,4},{6,7},{7,6},{8,9},{9,8},{10,11... | collective-permute-start | bytes 1474568 | tf_op jit(solution)/shard_map/left_x1/ppermute | solution.py:283
  77.4 3.6 %collective-permute-start.10 = (bf16[96,2560]{1,0:T(8,128)(2,1)S(1)}, bf16[96,2560]{1,0:T(8,128)(2,1)S(1)}, u32[]{:S(2)}, u32[]{:S(2)}) collective-permute-start(bf16[96,2560]{1,0:T(8,128)(2,1)S(1)} %collective-permute-done.8.refs_5_), channel_id=1, source_target_pairs={{0,1},{1,0},{2,3},{3,2},{4,5},{5,4},{6,7},{7,6},{8,9},{9,8},{10,11... | collective-permute-start | bytes 1474568 | tf_op jit(solution)/shard_map/right_x1/ppermute | solution.py:283
  77.8 16.9 %collective-permute-start.11 = (bf16[96,2560]{1,0:T(8,128)(2,1)}, bf16[96,2560]{1,0:T(8,128)(2,1)S(1)}, u32[]{:S(2)}, u32[]{:S(2)}) collective-permute-start(bf16[96,2560]{1,0:T(8,128)(2,1)} %collective-permute-done.3.refs_0_), channel_id=1, source_target_pairs={{0,2},{1,3},{2,4},{3,5},{4,6},{5,7},{6,0},{7,1},{8,10},{9,11},{10,... | collective-permute-start | bytes 1474568 | tf_op jit(solution)/shard_map/far0/ppermute | solution.py:279
  80.3 14.5 %collective-permute-start.14 = (bf16[96,2560]{1,0:T(8,128)(2,1)S(1)}, bf16[96,2560]{1,0:T(8,128)(2,1)S(1)}, u32[]{:S(2)}, u32[]{:S(2)}) collective-permute-start(bf16[96,2560]{1,0:T(8,128)(2,1)S(1)} %collective-permute-done.8.refs_5_), channel_id=1, source_target_pairs={{0,6},{1,7},{2,0},{3,1},{4,2},{5,3},{6,4},{7,5},{8,14},{9,15},{10,... | collective-permute-start | bytes 1474568 | tf_op jit(solution)/shard_map/far1/ppermute | solution.py:279
  93.4 4.6 %copy-start.12 = (bf16[192,2560]{1,0:T(8,128)(2,1)}, bf16[192,2560]{1,0:T(8,128)(2,1)S(1)}, u32[]{:S(2)}) copy-start(bf16[192,2560]{1,0:T(8,128)(2,1)S(1)} %get-tuple-element.58.refs_0_) | copy-start | bytes 2949124
  93.4 2.7 %collective-permute-start.12 = (bf16[192,2560]{1,0:T(8,128)(2,1)S(1)}, bf16[192,2560]{1,0:T(8,128)(2,1)S(1)}, u32[]{:S(2)}, u32[]{:S(2)}) collective-permute-start(bf16[192,2560]{1,0:T(8,128)(2,1)S(1)} %get-tuple-element.49), channel_id=1, source_target_pairs={{0,1},{1,0},{2,3},{3,2},{4,5},{5,4},{6,7},{7,6},{8,9},{9,8},{10,11... | collective-permute-start | bytes 2949128 | tf_op jit(solution)/shard_map/left_sum/ppermute | solution.py:283
  93.6 4.3 %collective-permute-start.13 = (bf16[192,2560]{1,0:T(8,128)(2,1)S(1)}, bf16[192,2560]{1,0:T(8,128)(2,1)S(1)}, u32[]{:S(2)}, u32[]{:S(2)}) collective-permute-start(bf16[192,2560]{1,0:T(8,128)(2,1)S(1)} %get-tuple-element.50), channel_id=1, source_target_pairs={{0,1},{1,0},{2,3},{3,2},{4,5},{5,4},{6,7},{7,6},{8,9},{9,8},{10,11... | collective-permute-start | bytes 2949128 | tf_op jit(solution)/shard_map/right_sum/ppermute | solution.py:283
  94.8 5.0 %collective-permute-start.15 = (bf16[96,2560]{1,0:T(8,128)(2,1)S(1)}, bf16[96,2560]{1,0:T(8,128)(2,1)S(1)}, u32[]{:S(2)}, u32[]{:S(2)}) collective-permute-start(bf16[96,2560]{1,0:T(8,128)(2,1)S(1)} %collective-permute-done.11.refs_0_), channel_id=1, source_target_pairs={{0,1},{1,0},{2,3},{3,2},{4,5},{5,4},{6,7},{7,6},{8,9},{9,8},{10,11... | collective-permute-start | bytes 1474568 | tf_op jit(solution)/shard_map/far_x0/ppermute | solution.py:283
  94.8 5.0 %collective-permute-start.16 = (bf16[96,2560]{1,0:T(8,128)(2,1)S(1)}, bf16[96,2560]{1,0:T(8,128)(2,1)S(1)}, u32[]{:S(2)}, u32[]{:S(2)}) collective-permute-start(bf16[96,2560]{1,0:T(8,128)(2,1)S(1)} %collective-permute-done.14.refs_1_), channel_id=1, source_target_pairs={{0,1},{1,0},{2,3},{3,2},{4,5},{5,4},{6,7},{7,6},{8,9},{9,8},{10,11... | collective-permute-start | bytes 1474568 | tf_op jit(solution)/shard_map/far_x1/ppermute | solution.py:283
  98.0 1.1 copy-start.14
  108.7 3.4 %collective-permute-start.17 = (bf16[192,2560]{1,0:T(8,128)(2,1)}, bf16[192,2560]{1,0:T(8,128)(2,1)S(1)}, u32[]{:S(2)}, u32[]{:S(2)}) collective-permute-start(bf16[192,2560]{1,0:T(8,128)(2,1)} %copy-done.28), channel_id=1, source_target_pairs={{0,1},{1,0},{2,3},{3,2},{4,5},{5,4},{6,7},{7,6},{8,9},{9,8},{10,11... | collective-permute-start | bytes 2949128 | tf_op jit(solution)/shard_map/far_sum/ppermute | solution.py:283
  108.8 15.3 %collective-permute-start.18 = (bf16[96,2560]{1,0:T(8,128)(2,1)S(1)}, bf16[96,2560]{1,0:T(8,128)(2,1)S(1)}, u32[]{:S(2)}, u32[]{:S(2)}) collective-permute-start(bf16[96,2560]{1,0:T(8,128)(2,1)S(1)} %sum_left0.1), channel_id=1, source_target_pairs={{0,6},{1,7},{2,0},{3,1},{4,2},{5,3},{6,4},{7,5},{8,14},{9,15},{10,... | collective-permute-start | bytes 1474568 | tf_op jit(solution)/shard_map/to_left0/ppermute | solution.py:279
  108.8 15.3 %collective-permute-start.19 = (bf16[96,2560]{1,0:T(8,128)(2,1)}, bf16[96,2560]{1,0:T(8,128)(2,1)S(1)}, u32[]{:S(2)}, u32[]{:S(2)}) collective-permute-start(bf16[96,2560]{1,0:T(8,128)(2,1)} %copy-done.22), channel_id=1, source_target_pairs={{0,2},{1,3},{2,4},{3,5},{4,6},{5,7},{6,0},{7,1},{8,10},{9,11},{10,... | collective-permute-start | bytes 1474568 | tf_op jit(solution)/shard_map/to_right1/ppermute | solution.py:279
  112.1 1.2 copy-start.17
  113.3 20.3 %copy-start.13 = (bf16[192,2560]{1,0:T(8,128)(2,1)S(1)}, bf16[192,2560]{1,0:T(8,128)(2,1)}, u32[]{:S(2)}) copy-start(bf16[192,2560]{1,0:T(8,128)(2,1)} %copy-done.12) | copy-start | bytes 2949124
  113.3 20.3 %copy-start.15 = (bf16[192,2560]{1,0:T(8,128)(2,1)S(1)}, bf16[192,2560]{1,0:T(8,128)(2,1)}, u32[]{:S(2)}) copy-start(bf16[192,2560]{1,0:T(8,128)(2,1)} %copy-done.14) | copy-start | bytes 2949124
  114.1 24.4 %copy-start.9 = (bf16[192,2560]{1,0:T(8,128)(2,1)S(1)}, bf16[192,2560]{1,0:T(8,128)(2,1)}, u32[]{:S(2)}) copy-start(bf16[192,2560]{1,0:T(8,128)(2,1)} %copy-done.8) | copy-start | bytes 2949124
  114.1 24.4 %copy-start.11 = (bf16[192,2560]{1,0:T(8,128)(2,1)S(1)}, bf16[192,2560]{1,0:T(8,128)(2,1)}, u32[]{:S(2)}) copy-start(bf16[192,2560]{1,0:T(8,128)(2,1)} %copy-done.10) | copy-start | bytes 2949124
  114.1 19.5 %collective-permute-start.20 = (bf16[96,2560]{1,0:T(8,128)(2,1)S(1)}, bf16[96,2560]{1,0:T(8,128)(2,1)S(1)}, u32[]{:S(2)}, u32[]{:S(2)}) collective-permute-start(bf16[96,2560]{1,0:T(8,128)(2,1)S(1)} %sum_far0.1), channel_id=1, source_target_pairs={{0,2},{1,3},{2,4},{3,5},{4,6},{5,7},{6,0},{7,1},{8,10},{9,11},{10,... | collective-permute-start | bytes 1474568 | tf_op jit(solution)/shard_map/via_right/ppermute | solution.py:279
  116.8 21.6 %collective-permute-start.22 = (bf16[96,2560]{1,0:T(8,128)(2,1)S(1)}, bf16[96,2560]{1,0:T(8,128)(2,1)S(1)}, u32[]{:S(2)}, u32[]{:S(2)}) collective-permute-start(bf16[96,2560]{1,0:T(8,128)(2,1)S(1)} %sum_far1.1), channel_id=1, source_target_pairs={{0,6},{1,7},{2,0},{3,1},{4,2},{5,3},{6,4},{7,5},{8,14},{9,15},{10,... | collective-permute-start | bytes 1474568 | tf_op jit(solution)/shard_map/via_left/ppermute | solution.py:279
  117.2 22.5 %collective-permute-start.2 = (bf16[192,2560]{1,0:T(8,128)(2,1)}, bf16[192,2560]{1,0:T(8,128)(2,1)S(1)}, u32[]{:S(2)}, u32[]{:S(2)}) collective-permute-start(bf16[192,2560]{1,0:T(8,128)(2,1)} %copy-done.27), channel_id=1, source_target_pairs={{0,1},{1,0},{2,3},{3,2},{4,5},{5,4},{6,7},{7,6},{8,9},{9,8},{10,11... | collective-permute-start | bytes 2949128 | tf_op jit(solution)/shard_map/own_sum/ppermute | solution.py:283
  124.1 28.9 %copy-start.19 = (bf16[192,2560]{1,0:T(8,128)(2,1)S(1)}, bf16[192,2560]{1,0:T(8,128)(2,1)}, u32[]{:S(2)}) copy-start(bf16[192,2560]{1,0:T(8,128)(2,1)} %copy-done.18) | copy-start | bytes 2949124
  134.7 13.7 %collective-permute-start.21 = (bf16[96,2560]{1,0:T(8,128)(2,1)S(1)}, bf16[96,2560]{1,0:T(8,128)(2,1)S(1)}, u32[]{:S(2)}, u32[]{:S(2)}) collective-permute-start(bf16[96,2560]{1,0:T(8,128)(2,1)S(1)} %sum_right0.1), channel_id=1, source_target_pairs={{0,2},{1,3},{2,4},{3,5},{4,6},{5,7},{6,0},{7,1},{8,10},{9,11},{10,... | collective-permute-start | bytes 1474568 | tf_op jit(solution)/shard_map/to_right0/ppermute | solution.py:279
  139.6 13.4 %collective-permute-start.23 = (bf16[96,2560]{1,0:T(8,128)(2,1)S(1)}, bf16[96,2560]{1,0:T(8,128)(2,1)S(1)}, u32[]{:S(2)}, u32[]{:S(2)}) collective-permute-start(bf16[96,2560]{1,0:T(8,128)(2,1)S(1)} %sum_left1.1), channel_id=1, source_target_pairs={{0,6},{1,7},{2,0},{3,1},{4,2},{5,3},{6,4},{7,5},{8,14},{9,15},{10,... | collective-permute-start | bytes 1474568 | tf_op jit(solution)/shard_map/to_left1/ppermute | solution.py:279
  156.4 35.2 %all-to-all-start.2 = ((bf16[32,24,640]{2,1,0:T(8,128)(2,1)}), bf16[32,24,640]{2,1,0:T(8,128)(2,1)S(1)}, u32[]{:S(2)}, u32[]{:S(2)}) async-start(bf16[32,24,640]{2,1,0:T(8,128)(2,1)} %bitcast.13), calls=%async_computation.2 | async-start | bytes 1966080 | tf_op jit(solution)/shard_map/back/all_to_all | solution.py:249
  166.1 1.3 collective-permute-start.24
  167.4 3.8 %collective-permute-start.25 = (f32[1,2560]{1,0:T(1,128)S(1)}, f32[1,2560]{1,0:T(1,128)S(1)}, u32[]{:S(2)}, u32[]{:S(2)}) collective-permute-start(f32[1,2560]{1,0:T(1,128)S(1)} %add.47), channel_id=1, source_target_pairs={{0,2},{1,3},{2,0},{3,1},{4,6},{5,7},{6,4},{7,5},{8,10},{9,11},{10,... | collective-permute-start | bytes 30728 | tf_op jit(solution)/shard_map/ppermute | solution.py:327
  171.1 5.3 %collective-permute-start.26 = (f32[1,2560]{1,0:T(1,128)S(1)}, f32[1,2560]{1,0:T(1,128)S(1)}, u32[]{:S(2)}, u32[]{:S(2)}) collective-permute-start(f32[1,2560]{1,0:T(1,128)S(1)} %add.48), channel_id=1, source_target_pairs={{0,4},{1,5},{2,6},{3,7},{4,0},{5,1},{6,2},{7,3},{8,12},{9,13},{10,... | collective-permute-start | bytes 30728 | tf_op jit(solution)/shard_map/ppermute | solution.py:327
  192.5 18.6 %all-to-all-start.3 = ((f32[32,8,320]{2,1,0:T(8,128)}), f32[32,8,320]{2,1,0:T(8,128)S(1)}, u32[]{:S(2)}, u32[]{:S(2)}) async-start(f32[32,8,320]{2,1,0:T(8,128)} %broadcast_in_dim.8), calls=%async_computation.3 | async-start | bytes 786432 | tf_op jit(solution)/shard_map/all_to_all | solution.py:330
  (12 other events, 11.0 us)
where the time goes:
time: 213 us; the launch traced here: 212 us
  waiting for transfers between devices  93.6 us (44%)
  starting transfers between devices  50.7 us (24%)
  Pallas kernels  45.7 us (21%)
  local copies, waits for them, and re-layouts  20.1 us (9%)
    all_to_all x3, waiting for transfers between devices, exchange(): lax.all_to_all(shaped, axis, split_axis=0, concat_axis=0, tiled=True)  39.7 us
    ppermute x12, waiting for transfers between devices, shift(): lax.ppermute(x, 'etp', [(i, (i // 2 + by) % chips * 2 + i % 2) for i in r...  28.2 us
    all_to_all x3, starting transfers between devices, exchange(): lax.all_to_all(shaped, axis, split_axis=0, concat_axis=0, tiled=True)  26.7 us
    pallas_call x3, Pallas kernels, expert(): pl.pallas_call(functools.partial(expert_kernel, first, counts), in_specs=...  26.3 us
    unnamed x58, local copies, waits for them, and re-layouts  18.2 us
    ppermute x12, starting transfers between devices, shift(): lax.ppermute(x, 'etp', [(i, (i // 2 + by) % chips * 2 + i % 2) for i in r...  16 us
    all_to_all x1, waiting for transfers between devices, local(): lax.all_to_all(spread, 'expert', split_axis=0, concat_axis=0, tiled=True)  11.8 us
    ppermute x3, waiting for transfers between devices, local(): lax.ppermute(column, 'etp', [(i, i ^ bit) for i in range(n_etp)])  9.98 us
  transfers between devices with their start and end apart: 31, of which 14 were waited for; matrix products, arithmetic and copies ran while one was open for 0% of the time, Pallas kernels for 17%

commit v1 on v0

--- a/solution.py
+++ b/solution.py
@@ -190,7 +190,7 @@
 def token_kernel(router_ref, keep_ref, keep_r_ref, *refs):
     parts, toks, (out_ref, column_ref) = refs[:4], refs[4:6], refs[6:]
     router = router_ref[...].astype(F32)
-    column = 0.0
+    column, grads = 0.0, []
     rows = toks[0].shape[0]
     take = out_ref.shape[0] // 2
     for half in range(2):
@@ -204,10 +204,16 @@
         d_logit = jnp.sum(tok * grad, axis=1, keepdims=True) * score * (1.0 - score)
         token_grad = (score * grad + d_logit * router).astype(BF16)
         column = column + jnp.sum(d_logit * tok, axis=0, keepdims=True)
-        out_ref[half * take : (half + 1) * take, :] = pack_rows(
-            token_grad, iota((1, rows), 1), rows // CAP, tuple(range(GROUPS))
-        )
+        grads.append(token_grad)
     column_ref[...] = column
+    width = out_ref.shape[1]
+    packed = [0.0, 0.0]
+    for piece in range(PIECES):
+        hot = hot_rows(iota((1, rows), 1), rows // CAP, tuple(range(GROUPS)), piece)
+        for half in range(2):
+            packed[half] = packed[half] + dot(hot, grads[half][:, piece * width : (piece + 1) * width])
+    for half in range(2):
+        out_ref[half * take : (half + 1) * take, :] = packed[half].astype(BF16)
 
 
 def token_math(kept, parts, tok, router, name):
@@ -326,9 +332,10 @@
     while bit < n_etp:
         column = column + lax.ppermute(column, "etp", [(i, i ^ bit) for i in range(n_etp)])
         bit *= 2
-    spread = jnp.broadcast_to(after(column, returned).reshape(1, TILE, width // TILE), (n_expert, TILE, width // TILE))
+    column = after(column, returned).astype(BF16).reshape(1, PIECES, width // PIECES)
+    spread = jnp.broadcast_to(column, (n_expert, PIECES, width // PIECES))
     spread = lax.all_to_all(spread, "expert", split_axis=0, concat_axis=0, tiled=True)
-    return (token_grad, spread.reshape(experts, width).T)
+    return (token_grad, spread.reshape(experts, width).astype(F32).T)
 
 
 def solution(mesh):

time: 213 us -> 210 us (0.986)
  waiting for transfers between devices: 93.6 us -> 90.7 us
    all_to_all x1, waiting for transfers between devices: 11.8 us -> 8.92 us  [local(): lax.all_to_all(spread, 'expert', split_axis=0, concat_axis=0, tiled=True)]
    unnamed x58 -> x59, local copies, waits for them, and re-layouts: 18.2 us -> 19 us
  transfers between devices with their start and end apart: 31 -> 31, of which waited for: 14 -> 14; matrix products, arithmetic and copies ran while one was open for 0% -> 0% of each run, Pallas kernels for 17% -> 18%
where the time goes in v1:
time: 210 us; the launch traced here: 209 us
  waiting for transfers between devices  90.7 us (43%)
  starting transfers between devices  50.7 us (24%)
  Pallas kernels  45.6 us (22%)
  local copies, waits for them, and re-layouts  19.9 us (9%)
    all_to_all x3, waiting for transfers between devices, exchange(): lax.all_to_all(shaped, axis, split_axis=0, concat_axis=0, tiled=True)  39.7 us
    ppermute x12, waiting for transfers between devices, shift(): lax.ppermute(x, 'etp', [(i, (i // 2 + by) % chips * 2 + i % 2) for i in r...  28.2 us
    all_to_all x3, starting transfers between devices, exchange(): lax.all_to_all(shaped, axis, split_axis=0, concat_axis=0, tiled=True)  26.7 us
    pallas_call x3, Pallas kernels, expert(): pl.pallas_call(functools.partial(expert_kernel, first, counts), in_specs=...  26.3 us
    unnamed x59, local copies, waits for them, and re-layouts  19 us
    ppermute x12, starting transfers between devices, shift(): lax.ppermute(x, 'etp', [(i, (i // 2 + by) % chips * 2 + i % 2) for i in r...  16 us
    ppermute x3, waiting for transfers between devices, local(): lax.ppermute(column, 'etp', [(i, i ^ bit) for i in range(n_etp)])  9.98 us
    all_to_all x1, waiting for transfers between devices, local(): lax.all_to_all(spread, 'expert', split_axis=0, concat_axis=0, tiled=True)  8.92 us
  transfers between devices with their start and end apart: 31, of which 14 were waited for; matrix products, arithmetic and copies ran while one was open for 0% of the time, Pallas kernels for 18%

profile of v1, /device:TPU:6, one launch (start us, length us, event | category | flops | bytes accessed | tf_op | source)
XLA Modules:
  0.0 208.8 jit_solution(15152822400399524180)
XLA Ops:
  1.6 1.1 copy-done.20
  3.4 2.3 %pack_grad.1 = bf16[768,640]{1,0:T(8,128)(2,1)} custom-call(s32[1,128]{1,0:T(1,128)S(1)} %bitcast.40, bf16[128,2560]{1,0:T(8,128)(2,1)S(1)} %copy-done.20), custom_call_target="tpu_custom_call" | custom-call | bytes 1048576 | tf_op jit(solution)/shard_map/pack_grad/pallas_call | solution.py:65
  5.7 11.6 %all-to-all-start = ((bf16[32,24,640]{2,1,0:T(8,128)(2,1)}), bf16[32,24,640]{2,1,0:T(8,128)(2,1)}, u32[]{:S(2)}, u32[]{:S(2)}) async-start(bf16[32,24,640]{2,1,0:T(8,128)(2,1)} %bitcast.4), calls=%async_computation | async-start | bytes 1966080 | tf_op jit(solution)/shard_map/grads/all_to_all | solution.py:255
  17.3 1.3 pack_tok.1
  18.6 1.0 copy-done.7
  19.6 24.5 %all-to-all-done = bf16[32,24,640]{2,1,0:T(8,128)(2,1)} async-done(((bf16[32,24,640]{2,1,0:T(8,128)(2,1)}), bf16[32,24,640]{2,1,0:T(8,128)(2,1)}, u32[]{:S(2)}, u32[]{:S(2)}) %all-to-all-start) | async-done | bytes 983072 | tf_op jit(solution)/shard_map/grads/all_to_all | solution.py:255
  44.2 3.1 %unpack_grad.1 = (bf16[96,2560]{1,0:T(8,128)(2,1)}, bf16[96,2560]{1,0:T(8,128)(2,1)}) custom-call(bf16[768,640]{1,0:T(8,128)(2,1)} %bitcast.5.packed_ref), custom_call_target="tpu_custom_call" | custom-call | bytes 1048576 | tf_op jit(solution)/shard_map/unpack_grad/pallas_call | solution.py:88
  47.7 0.8 collective-permute-start.8
  48.5 2.4 %collective-permute-start.3 = (bf16[96,2560]{1,0:T(8,128)(2,1)}, bf16[96,2560]{1,0:T(8,128)(2,1)}, u32[]{:S(2)}, u32[]{:S(2)}) collective-permute-start(bf16[96,2560]{1,0:T(8,128)(2,1)} %get-tuple-element.39.refs_0_), channel_id=1, source_target_pairs={{0,2},{1,3},{2,4},{3,5},{4,6},{5,7},{6,0},{7,1},{8,10},{9,11},{10,... | collective-permute-start | bytes 1474568 | tf_op jit(solution)/shard_map/left0/ppermute | solution.py:285
  51.0 0.8 copy-done.23
  51.8 3.2 %collective-permute-start.4 = (bf16[96,2560]{1,0:T(8,128)(2,1)}, bf16[96,2560]{1,0:T(8,128)(2,1)}, u32[]{:S(2)}, u32[]{:S(2)}) collective-permute-start(bf16[96,2560]{1,0:T(8,128)(2,1)} %get-tuple-element.40.refs_1_), channel_id=1, source_target_pairs={{0,2},{1,3},{2,4},{3,5},{4,6},{5,7},{6,0},{7,1},{8,10},{9,11},{10,... | collective-permute-start | bytes 1474568 | tf_op jit(solution)/shard_map/left1/ppermute | solution.py:285
  55.0 5.4 %all-to-all-start.1 = ((bf16[32,24,640]{2,1,0:T(8,128)(2,1)}), bf16[32,24,640]{2,1,0:T(8,128)(2,1)}, u32[]{:S(2)}, u32[]{:S(2)}) async-start(bf16[32,24,640]{2,1,0:T(8,128)(2,1)} %bitcast.38), calls=%async_computation.1 | async-start | bytes 1966080 | tf_op jit(solution)/shard_map/toks/all_to_all | solution.py:255
  60.5 1.7 copy-done.2
  62.2 1.7 copy-done.3
  64.0 1.4 copy-done.4
  65.4 1.4 copy-done.6
  66.8 1.0 copy-done.24
  67.8 7.1 %expert_own.1 = (bf16[192,2560]{1,0:T(8,128)(2,1)S(1)}, bf16[192,2560]{1,0:T(8,128)(2,1)S(1)}) custom-call(s32[8]{0:T(128)S(1)} %reshape.41.ids_ref, bf16[96,2560]{1,0:T(8,128)(2,1)} %get-tuple-element.39.refs_0_, bf16[96,2560]{1,0:T(8,128)(2,1)} %get-tuple-element.40.refs_1_, bf16[96,2560]{1,0:T(8,128)(2,1)S(1)} %copy-done.24, ...), custom_call_target="tpu_custom_call" | custom-call | bytes 1048576 | tf_op jit(solution)/shard_map/expert_own/pallas_call | solution.py:150
  74.9 1.0 copy-done.18
  75.8 1.0 copy-done.27
  77.9 2.4 %collective-permute-done.9.refs_6_ = bf16[96,2560]{1,0:T(8,128)(2,1)S(1)} collective-permute-done((bf16[96,2560]{1,0:T(8,128)(2,1)}, bf16[96,2560]{1,0:T(8,128)(2,1)S(1)}, u32[]{:S(2)}, u32[]{:S(2)}) %collective-permute-start.9) | collective-permute-done | bytes 491552 | tf_op jit(solution)/shard_map/right_x0/ppermute | solution.py:289
  81.0 12.4 %expert_sides.1 = (bf16[192,2560]{1,0:T(8,128)(2,1)S(1)}, bf16[192,2560]{1,0:T(8,128)(2,1)S(1)}, bf16[192,2560]{1,0:T(8,128)(2,1)S(1)}, bf16[192,2560]{1,0:T(8,128)(2,1)S(1)}) custom-call(s32[8]{0:T(128)S(1)} %reshape.41.ids_ref, bf16[96,2560]{1,0:T(8,128)(2,1)} %collective-permute-done.3.refs_0_, bf16[96,2560]{1,0:T(8,128)(2,1)} %collective-permute-done.4.refs_1_, ...), custom_call_target="tpu_custom_call" | custom-call | bytes 1048576 | tf_op jit(solution)/shard_map/expert_sides/pallas_call | solution.py:150
  94.0 0.8 collective-permute-done.14.refs_1_
  97.0 0.9 copy-done.8
  99.0 0.8 copy-done.22
  99.8 6.9 %expert_far.1 = (bf16[192,2560]{1,0:T(8,128)(2,1)S(1)}, bf16[192,2560]{1,0:T(8,128)(2,1)S(1)}) custom-call(s32[8]{0:T(128)S(1)} %reshape.41.ids_ref, bf16[96,2560]{1,0:T(8,128)(2,1)S(1)} %collective-permute-done.11.refs_0_, bf16[96,2560]{1,0:T(8,128)(2,1)S(1)} %collective-permute-done.14.refs_1_, bf16[96,2560]{1,0:T(8,128)(2,1)S(1)} %collective-permute-done.15.refs_2_, ...), custom_call_target="tpu_custom_call" | custom-call | bytes 1048576 | tf_op jit(solution)/shard_map/expert_far/pallas_call | solution.py:150
  106.7 1.0 copy-done.16
  107.7 1.0 copy-done.28
  108.8 3.2 %collective-permute-start.19 = (bf16[96,2560]{1,0:T(8,128)(2,1)}, bf16[96,2560]{1,0:T(8,128)(2,1)S(1)}, u32[]{:S(2)}, u32[]{:S(2)}) collective-permute-start(bf16[96,2560]{1,0:T(8,128)(2,1)} %copy-done.22), channel_id=1, source_target_pairs={{0,2},{1,3},{2,4},{3,5},{4,6},{5,7},{6,0},{7,1},{8,10},{9,11},{10,... | collective-permute-start | bytes 1474568 | tf_op jit(solution)/shard_map/to_right1/ppermute | solution.py:285
  112.1 1.2 copy-done.17
  114.1 2.0 collective-permute-start.20
  117.3 2.1 %unpack_tok.1 = (bf16[96,2560]{1,0:T(8,128)(2,1)S(1)}, bf16[96,2560]{1,0:T(8,128)(2,1)S(1)}) custom-call(bf16[768,640]{1,0:T(8,128)(2,1)} %bitcast.12.packed_ref), custom_call_target="tpu_custom_call" | custom-call | bytes 1048576 | tf_op jit(solution)/shard_map/unpack_tok/pallas_call | solution.py:88
  119.4 4.7 %collective-permute-done.18.refs_1_ = bf16[96,2560]{1,0:T(8,128)(2,1)S(1)} collective-permute-done((bf16[96,2560]{1,0:T(8,128)(2,1)S(1)}, bf16[96,2560]{1,0:T(8,128)(2,1)S(1)}, u32[]{:S(2)}, u32[]{:S(2)}) %collective-permute-start.18) | collective-permute-done | bytes 491552 | tf_op jit(solution)/shard_map/to_left0/ppermute | solution.py:285
  124.1 9.4 %collective-permute-done.20.refs_2_ = bf16[96,2560]{1,0:T(8,128)(2,1)S(1)} collective-permute-done((bf16[96,2560]{1,0:T(8,128)(2,1)S(1)}, bf16[96,2560]{1,0:T(8,128)(2,1)S(1)}, u32[]{:S(2)}, u32[]{:S(2)}) %collective-permute-start.20) | collective-permute-done | bytes 491552 | tf_op jit(solution)/shard_map/via_right/ppermute | solution.py:285
  133.6 1.1 sum_right0.1
  134.7 3.8 %collective-permute-start.21 = (bf16[96,2560]{1,0:T(8,128)(2,1)S(1)}, bf16[96,2560]{1,0:T(8,128)(2,1)S(1)}, u32[]{:S(2)}, u32[]{:S(2)}) collective-permute-start(bf16[96,2560]{1,0:T(8,128)(2,1)S(1)} %sum_right0.1), channel_id=1, source_target_pairs={{0,2},{1,3},{2,4},{3,5},{4,6},{5,7},{6,0},{7,1},{8,10},{9,11},{10,... | collective-permute-start | bytes 1474568 | tf_op jit(solution)/shard_map/to_right0/ppermute | solution.py:285
  138.5 1.1 sum_left1.1
  139.7 8.6 %collective-permute-done.21.refs_0_ = bf16[96,2560]{1,0:T(8,128)(2,1)S(1)} collective-permute-done((bf16[96,2560]{1,0:T(8,128)(2,1)S(1)}, bf16[96,2560]{1,0:T(8,128)(2,1)S(1)}, u32[]{:S(2)}, u32[]{:S(2)}) %collective-permute-start.21) | collective-permute-done | bytes 491552 | tf_op jit(solution)/shard_map/to_right0/ppermute | solution.py:285
  148.4 4.7 %collective-permute-done.23.refs_3_ = bf16[96,2560]{1,0:T(8,128)(2,1)S(1)} collective-permute-done((bf16[96,2560]{1,0:T(8,128)(2,1)S(1)}, bf16[96,2560]{1,0:T(8,128)(2,1)S(1)}, u32[]{:S(2)}, u32[]{:S(2)}) %collective-permute-start.23) | collective-permute-done | bytes 491552 | tf_op jit(solution)/shard_map/to_left1/ppermute | solution.py:285
  153.0 3.3 %token_math.1 = (bf16[768,640]{1,0:T(8,128)(2,1)}, f32[1,2560]{1,0:T(1,128)S(1)}) custom-call(bf16[1,2560]{1,0:T(2,128)(2,1)S(1)} %dynamic-slice_bitcast_fusion.router_ref, bf16[192,2560]{1,0:T(8,128)(2,1)S(1)} %copy-done.19, bf16[192,2560]{1,0:T(8,128)(2,1)S(1)} %collective-permute-done.2.keep_r_ref, bf16[96,2560]{1,0:T(8,128)(2,1)S(1)} %collective-permute-done.21.refs_0_, ...), custom_call_target="tpu_custom_call" | custom-call | bytes 1048576 | tf_op jit(solution)/shard_map/token_math/pallas_call | solution.py:221
  156.4 9.7 %all-to-all-start.2 = ((bf16[32,24,640]{2,1,0:T(8,128)(2,1)}), bf16[32,24,640]{2,1,0:T(8,128)(2,1)S(1)}, u32[]{:S(2)}, u32[]{:S(2)}) async-start(bf16[32,24,640]{2,1,0:T(8,128)(2,1)} %bitcast.13), calls=%async_computation.2 | async-start | bytes 1966080 | tf_op jit(solution)/shard_map/back/all_to_all | solution.py:255
  166.2 1.2 collective-permute-done.24
  167.4 3.7 %collective-permute-done.25 = f32[1,2560]{1,0:T(1,128)S(1)} collective-permute-done((f32[1,2560]{1,0:T(1,128)S(1)}, f32[1,2560]{1,0:T(1,128)S(1)}, u32[]{:S(2)}, u32[]{:S(2)}) %collective-permute-start.25) | collective-permute-done | bytes 10272 | tf_op jit(solution)/shard_map/ppermute | solution.py:333
  171.2 5.2 %collective-permute-done.26 = f32[1,2560]{1,0:T(1,128)S(1)} collective-permute-done((f32[1,2560]{1,0:T(1,128)S(1)}, f32[1,2560]{1,0:T(1,128)S(1)}, u32[]{:S(2)}, u32[]{:S(2)}) %collective-permute-start.26) | collective-permute-done | bytes 10272 | tf_op jit(solution)/shard_map/ppermute | solution.py:333
  176.4 15.1 %all-to-all-done.2 = bf16[32,24,640]{2,1,0:T(8,128)(2,1)S(1)} async-done(((bf16[32,24,640]{2,1,0:T(8,128)(2,1)}), bf16[32,24,640]{2,1,0:T(8,128)(2,1)S(1)}, u32[]{:S(2)}, u32[]{:S(2)}) %all-to-all-start.2) | async-done | bytes 983072 | tf_op jit(solution)/shard_map/back/all_to_all | solution.py:255
  192.3 4.9 %all-to-all-start.3 = ((bf16[32,4,640]{2,1,0:T(4,128)(2,1)}), bf16[32,4,640]{2,1,0:T(4,128)(2,1)S(1)}, u32[]{:S(2)}, u32[]{:S(2)}) async-start(bf16[32,4,640]{2,1,0:T(4,128)(2,1)} %broadcast_in_dim.8), calls=%async_computation.3 | async-start | bytes 327680 | tf_op jit(solution)/shard_map/all_to_all | solution.py:337
  197.2 1.8 final.1
  199.1 8.9 %all-to-all-done.3 = bf16[32,4,640]{2,1,0:T(4,128)(2,1)S(1)} async-done(((bf16[32,4,640]{2,1,0:T(4,128)(2,1)}), bf16[32,4,640]{2,1,0:T(4,128)(2,1)S(1)}, u32[]{:S(2)}, u32[]{:S(2)}) %all-to-all-start.3) | async-done | bytes 163872 | tf_op jit(solution)/shard_map/all_to_all | solution.py:337
  (100 shorter events, 11.8 us)
Async XLA Ops:
  0.6 16.6 %copy-start.26 = (s32[128,1]{0,1:T(1,128)S(1)}, s32[128,1]{0,1:T(1,128)}, u32[]{:S(2)}) copy-start(s32[128,1]{0,1:T(1,128)} %param.13) | copy-start | bytes 1540
  1.6 1.1 copy-start.20
  3.4 13.9 %copy-start.21 = (bf16[128,2560]{1,0:T(8,128)(2,1)S(1)}, bf16[128,2560]{1,0:T(8,128)(2,1)}, u32[]{:S(2)}) copy-start(bf16[128,2560]{1,0:T(8,128)(2,1)} %rows_ref.2) | copy-start | bytes 1966084
  5.7 38.5 %all-to-all-start = ((bf16[32,24,640]{2,1,0:T(8,128)(2,1)}), bf16[32,24,640]{2,1,0:T(8,128)(2,1)}, u32[]{:S(2)}, u32[]{:S(2)}) async-start(bf16[32,24,640]{2,1,0:T(8,128)(2,1)} %bitcast.4), calls=%async_computation | async-start | bytes 1966080 | tf_op jit(solution)/shard_map/grads/all_to_all | solution.py:255
  17.3 43.2 %copy-start.1 = (bf16[1,512,2560]{2,1,0:T(8,128)(2,1)S(1)}, bf16[1,512,2560]{2,1,0:T(8,128)(2,1)}, u32[]{:S(2)}) copy-start(bf16[1,512,2560]{2,1,0:T(8,128)(2,1)} %param.18) | copy-start | bytes 7864324
  47.2 3.8 %collective-permute-start = (bf16[96,2560]{1,0:T(8,128)(2,1)}, bf16[96,2560]{1,0:T(8,128)(2,1)S(1)}, u32[]{:S(2)}, u32[]{:S(2)}) collective-permute-start(bf16[96,2560]{1,0:T(8,128)(2,1)} %get-tuple-element.39.refs_0_), channel_id=1, source_target_pairs={{0,1},{1,0},{2,3},{3,2},{4,5},{5,4},{6,7},{7,6},{8,9},{9,8},{10,11... | collective-permute-start | bytes 1474568 | tf_op jit(solution)/shard_map/own_x0/ppermute | solution.py:289
  47.2 13.2 %collective-permute-start.1 = (bf16[96,2560]{1,0:T(8,128)(2,1)}, bf16[96,2560]{1,0:T(8,128)(2,1)}, u32[]{:S(2)}, u32[]{:S(2)}) collective-permute-start(bf16[96,2560]{1,0:T(8,128)(2,1)} %get-tuple-element.40.refs_1_), channel_id=1, source_target_pairs={{0,1},{1,0},{2,3},{3,2},{4,5},{5,4},{6,7},{7,6},{8,9},{9,8},{10,11... | collective-permute-start | bytes 1474568 | tf_op jit(solution)/shard_map/own_x1/ppermute | solution.py:289
  47.7 29.1 %collective-permute-start.8 = (bf16[96,2560]{1,0:T(8,128)(2,1)}, bf16[96,2560]{1,0:T(8,128)(2,1)S(1)}, u32[]{:S(2)}, u32[]{:S(2)}) collective-permute-start(bf16[96,2560]{1,0:T(8,128)(2,1)} %get-tuple-element.40.refs_1_), channel_id=1, source_target_pairs={{0,6},{1,7},{2,0},{3,1},{4,2},{5,3},{6,4},{7,5},{8,14},{9,15},{10,... | collective-permute-start | bytes 1474568 | tf_op jit(solution)/shard_map/right1/ppermute | solution.py:285
  48.5 28.3 %collective-permute-start.3 = (bf16[96,2560]{1,0:T(8,128)(2,1)}, bf16[96,2560]{1,0:T(8,128)(2,1)}, u32[]{:S(2)}, u32[]{:S(2)}) collective-permute-start(bf16[96,2560]{1,0:T(8,128)(2,1)} %get-tuple-element.39.refs_0_), channel_id=1, source_target_pairs={{0,2},{1,3},{2,4},{3,5},{4,6},{5,7},{6,0},{7,1},{8,10},{9,11},{10,... | collective-permute-start | bytes 1474568 | tf_op jit(solution)/shard_map/left0/ppermute | solution.py:285
  51.0 25.9 %collective-permute-start.7 = (bf16[96,2560]{1,0:T(8,128)(2,1)}, bf16[96,2560]{1,0:T(8,128)(2,1)}, u32[]{:S(2)}, u32[]{:S(2)}) collective-permute-start(bf16[96,2560]{1,0:T(8,128)(2,1)} %get-tuple-element.39.refs_0_), channel_id=1, source_target_pairs={{0,6},{1,7},{2,0},{3,1},{4,2},{5,3},{6,4},{7,5},{8,14},{9,15},{10,... | collective-permute-start | bytes 1474568 | tf_op jit(solution)/shard_map/right0/ppermute | solution.py:285
  51.8 25.6 %collective-permute-start.4 = (bf16[96,2560]{1,0:T(8,128)(2,1)}, bf16[96,2560]{1,0:T(8,128)(2,1)}, u32[]{:S(2)}, u32[]{:S(2)}) collective-permute-start(bf16[96,2560]{1,0:T(8,128)(2,1)} %get-tuple-element.40.refs_1_), channel_id=1, source_target_pairs={{0,2},{1,3},{2,4},{3,5},{4,6},{5,7},{6,0},{7,1},{8,10},{9,11},{10,... | collective-permute-start | bytes 1474568 | tf_op jit(solution)/shard_map/left1/ppermute | solution.py:285
  55.0 53.7 %all-to-all-start.1 = ((bf16[32,24,640]{2,1,0:T(8,128)(2,1)}), bf16[32,24,640]{2,1,0:T(8,128)(2,1)}, u32[]{:S(2)}, u32[]{:S(2)}) async-start(bf16[32,24,640]{2,1,0:T(8,128)(2,1)} %bitcast.38), calls=%async_computation.1 | async-start | bytes 1966080 | tf_op jit(solution)/shard_map/toks/all_to_all | solution.py:255
  60.5 1.7 copy-start.2
  62.2 1.7 copy-start.3
  64.0 1.4 copy-start.4
  65.4 1.4 copy-start.6
  67.8 13.2 %copy-start.5 = (bf16[1,1536,512]{2,1,0:T(8,128)(2,1)S(1)}, bf16[1,1536,512]{2,1,0:T(8,128)(2,1)}, u32[]{:S(2)}) copy-start(bf16[1,1536,512]{2,1,0:T(8,128)(2,1)} %param.14) | copy-start | bytes 4718596
  76.8 4.2 %collective-permute-start.5 = (bf16[96,2560]{1,0:T(8,128)(2,1)}, bf16[96,2560]{1,0:T(8,128)(2,1)S(1)}, u32[]{:S(2)}, u32[]{:S(2)}) collective-permute-start(bf16[96,2560]{1,0:T(8,128)(2,1)} %collective-permute-done.3.refs_0_), channel_id=1, source_target_pairs={{0,1},{1,0},{2,3},{3,2},{4,5},{5,4},{6,7},{7,6},{8,9},{9,8},{10,11... | collective-permute-start | bytes 1474568 | tf_op jit(solution)/shard_map/left_x0/ppermute | solution.py:289
  76.8 3.5 %collective-permute-start.9 = (bf16[96,2560]{1,0:T(8,128)(2,1)}, bf16[96,2560]{1,0:T(8,128)(2,1)S(1)}, u32[]{:S(2)}, u32[]{:S(2)}) collective-permute-start(bf16[96,2560]{1,0:T(8,128)(2,1)} %collective-permute-done.7.refs_4_), channel_id=1, source_target_pairs={{0,1},{1,0},{2,3},{3,2},{4,5},{5,4},{6,7},{7,6},{8,9},{9,8},{10,11... | collective-permute-start | bytes 1474568 | tf_op jit(solution)/shard_map/right_x0/ppermute | solution.py:289
  77.3 3.7 %collective-permute-start.6 = (bf16[96,2560]{1,0:T(8,128)(2,1)}, bf16[96,2560]{1,0:T(8,128)(2,1)S(1)}, u32[]{:S(2)}, u32[]{:S(2)}) collective-permute-start(bf16[96,2560]{1,0:T(8,128)(2,1)} %collective-permute-done.4.refs_1_), channel_id=1, source_target_pairs={{0,1},{1,0},{2,3},{3,2},{4,5},{5,4},{6,7},{7,6},{8,9},{9,8},{10,11... | collective-permute-start | bytes 1474568 | tf_op jit(solution)/shard_map/left_x1/ppermute | solution.py:289
  77.4 3.6 %collective-permute-start.10 = (bf16[96,2560]{1,0:T(8,128)(2,1)S(1)}, bf16[96,2560]{1,0:T(8,128)(2,1)S(1)}, u32[]{:S(2)}, u32[]{:S(2)}) collective-permute-start(bf16[96,2560]{1,0:T(8,128)(2,1)S(1)} %collective-permute-done.8.refs_5_), channel_id=1, source_target_pairs={{0,1},{1,0},{2,3},{3,2},{4,5},{5,4},{6,7},{7,6},{8,9},{9,8},{10,11... | collective-permute-start | bytes 1474568 | tf_op jit(solution)/shard_map/right_x1/ppermute | solution.py:289
  77.8 16.9 %collective-permute-start.11 = (bf16[96,2560]{1,0:T(8,128)(2,1)}, bf16[96,2560]{1,0:T(8,128)(2,1)S(1)}, u32[]{:S(2)}, u32[]{:S(2)}) collective-permute-start(bf16[96,2560]{1,0:T(8,128)(2,1)} %collective-permute-done.3.refs_0_), channel_id=1, source_target_pairs={{0,2},{1,3},{2,4},{3,5},{4,6},{5,7},{6,0},{7,1},{8,10},{9,11},{10,... | collective-permute-start | bytes 1474568 | tf_op jit(solution)/shard_map/far0/ppermute | solution.py:285
  80.3 14.5 %collective-permute-start.14 = (bf16[96,2560]{1,0:T(8,128)(2,1)S(1)}, bf16[96,2560]{1,0:T(8,128)(2,1)S(1)}, u32[]{:S(2)}, u32[]{:S(2)}) collective-permute-start(bf16[96,2560]{1,0:T(8,128)(2,1)S(1)} %collective-permute-done.8.refs_5_), channel_id=1, source_target_pairs={{0,6},{1,7},{2,0},{3,1},{4,2},{5,3},{6,4},{7,5},{8,14},{9,15},{10,... | collective-permute-start | bytes 1474568 | tf_op jit(solution)/shard_map/far1/ppermute | solution.py:285
  93.4 4.6 %copy-start.12 = (bf16[192,2560]{1,0:T(8,128)(2,1)}, bf16[192,2560]{1,0:T(8,128)(2,1)S(1)}, u32[]{:S(2)}) copy-start(bf16[192,2560]{1,0:T(8,128)(2,1)S(1)} %get-tuple-element.58.refs_0_) | copy-start | bytes 2949124
  93.4 2.7 %collective-permute-start.12 = (bf16[192,2560]{1,0:T(8,128)(2,1)S(1)}, bf16[192,2560]{1,0:T(8,128)(2,1)S(1)}, u32[]{:S(2)}, u32[]{:S(2)}) collective-permute-start(bf16[192,2560]{1,0:T(8,128)(2,1)S(1)} %get-tuple-element.49), channel_id=1, source_target_pairs={{0,1},{1,0},{2,3},{3,2},{4,5},{5,4},{6,7},{7,6},{8,9},{9,8},{10,11... | collective-permute-start | bytes 2949128 | tf_op jit(solution)/shard_map/left_sum/ppermute | solution.py:289
  93.6 4.3 %collective-permute-start.13 = (bf16[192,2560]{1,0:T(8,128)(2,1)S(1)}, bf16[192,2560]{1,0:T(8,128)(2,1)S(1)}, u32[]{:S(2)}, u32[]{:S(2)}) collective-permute-start(bf16[192,2560]{1,0:T(8,128)(2,1)S(1)} %get-tuple-element.50), channel_id=1, source_target_pairs={{0,1},{1,0},{2,3},{3,2},{4,5},{5,4},{6,7},{7,6},{8,9},{9,8},{10,11... | collective-permute-start | bytes 2949128 | tf_op jit(solution)/shard_map/right_sum/ppermute | solution.py:289
  94.8 5.0 %collective-permute-start.15 = (bf16[96,2560]{1,0:T(8,128)(2,1)S(1)}, bf16[96,2560]{1,0:T(8,128)(2,1)S(1)}, u32[]{:S(2)}, u32[]{:S(2)}) collective-permute-start(bf16[96,2560]{1,0:T(8,128)(2,1)S(1)} %collective-permute-done.11.refs_0_), channel_id=1, source_target_pairs={{0,1},{1,0},{2,3},{3,2},{4,5},{5,4},{6,7},{7,6},{8,9},{9,8},{10,11... | collective-permute-start | bytes 1474568 | tf_op jit(solution)/shard_map/far_x0/ppermute | solution.py:289
  94.8 5.0 %collective-permute-start.16 = (bf16[96,2560]{1,0:T(8,128)(2,1)S(1)}, bf16[96,2560]{1,0:T(8,128)(2,1)S(1)}, u32[]{:S(2)}, u32[]{:S(2)}) collective-permute-start(bf16[96,2560]{1,0:T(8,128)(2,1)S(1)} %collective-permute-done.14.refs_1_), channel_id=1, source_target_pairs={{0,1},{1,0},{2,3},{3,2},{4,5},{5,4},{6,7},{7,6},{8,9},{9,8},{10,11... | collective-permute-start | bytes 1474568 | tf_op jit(solution)/shard_map/far_x1/ppermute | solution.py:289
  98.0 1.1 copy-start.14
  108.7 3.4 %collective-permute-start.17 = (bf16[192,2560]{1,0:T(8,128)(2,1)}, bf16[192,2560]{1,0:T(8,128)(2,1)S(1)}, u32[]{:S(2)}, u32[]{:S(2)}) collective-permute-start(bf16[192,2560]{1,0:T(8,128)(2,1)} %copy-done.28), channel_id=1, source_target_pairs={{0,1},{1,0},{2,3},{3,2},{4,5},{5,4},{6,7},{7,6},{8,9},{9,8},{10,11... | collective-permute-start | bytes 2949128 | tf_op jit(solution)/shard_map/far_sum/ppermute | solution.py:289
  108.8 15.3 %collective-permute-start.18 = (bf16[96,2560]{1,0:T(8,128)(2,1)S(1)}, bf16[96,2560]{1,0:T(8,128)(2,1)S(1)}, u32[]{:S(2)}, u32[]{:S(2)}) collective-permute-start(bf16[96,2560]{1,0:T(8,128)(2,1)S(1)} %sum_left0.1), channel_id=1, source_target_pairs={{0,6},{1,7},{2,0},{3,1},{4,2},{5,3},{6,4},{7,5},{8,14},{9,15},{10,... | collective-permute-start | bytes 1474568 | tf_op jit(solution)/shard_map/to_left0/ppermute | solution.py:285
  108.8 15.3 %collective-permute-start.19 = (bf16[96,2560]{1,0:T(8,128)(2,1)}, bf16[96,2560]{1,0:T(8,128)(2,1)S(1)}, u32[]{:S(2)}, u32[]{:S(2)}) collective-permute-start(bf16[96,2560]{1,0:T(8,128)(2,1)} %copy-done.22), channel_id=1, source_target_pairs={{0,2},{1,3},{2,4},{3,5},{4,6},{5,7},{6,0},{7,1},{8,10},{9,11},{10,... | collective-permute-start | bytes 1474568 | tf_op jit(solution)/shard_map/to_right1/ppermute | solution.py:285
  112.1 1.2 copy-start.17
  113.3 20.3 %copy-start.13 = (bf16[192,2560]{1,0:T(8,128)(2,1)S(1)}, bf16[192,2560]{1,0:T(8,128)(2,1)}, u32[]{:S(2)}) copy-start(bf16[192,2560]{1,0:T(8,128)(2,1)} %copy-done.12) | copy-start | bytes 2949124
  113.3 20.3 %copy-start.15 = (bf16[192,2560]{1,0:T(8,128)(2,1)S(1)}, bf16[192,2560]{1,0:T(8,128)(2,1)}, u32[]{:S(2)}) copy-start(bf16[192,2560]{1,0:T(8,128)(2,1)} %copy-done.14) | copy-start | bytes 2949124
  114.1 24.4 %copy-start.9 = (bf16[192,2560]{1,0:T(8,128)(2,1)S(1)}, bf16[192,2560]{1,0:T(8,128)(2,1)}, u32[]{:S(2)}) copy-start(bf16[192,2560]{1,0:T(8,128)(2,1)} %copy-done.8) | copy-start | bytes 2949124
  114.1 24.4 %copy-start.11 = (bf16[192,2560]{1,0:T(8,128)(2,1)S(1)}, bf16[192,2560]{1,0:T(8,128)(2,1)}, u32[]{:S(2)}) copy-start(bf16[192,2560]{1,0:T(8,128)(2,1)} %copy-done.10) | copy-start | bytes 2949124
  114.1 19.5 %collective-permute-start.20 = (bf16[96,2560]{1,0:T(8,128)(2,1)S(1)}, bf16[96,2560]{1,0:T(8,128)(2,1)S(1)}, u32[]{:S(2)}, u32[]{:S(2)}) collective-permute-start(bf16[96,2560]{1,0:T(8,128)(2,1)S(1)} %sum_far0.1), channel_id=1, source_target_pairs={{0,2},{1,3},{2,4},{3,5},{4,6},{5,7},{6,0},{7,1},{8,10},{9,11},{10,... | collective-permute-start | bytes 1474568 | tf_op jit(solution)/shard_map/via_right/ppermute | solution.py:285
  116.8 21.6 %collective-permute-start.22 = (bf16[96,2560]{1,0:T(8,128)(2,1)S(1)}, bf16[96,2560]{1,0:T(8,128)(2,1)S(1)}, u32[]{:S(2)}, u32[]{:S(2)}) collective-permute-start(bf16[96,2560]{1,0:T(8,128)(2,1)S(1)} %sum_far1.1), channel_id=1, source_target_pairs={{0,6},{1,7},{2,0},{3,1},{4,2},{5,3},{6,4},{7,5},{8,14},{9,15},{10,... | collective-permute-start | bytes 1474568 | tf_op jit(solution)/shard_map/via_left/ppermute | solution.py:285
  117.2 22.5 %collective-permute-start.2 = (bf16[192,2560]{1,0:T(8,128)(2,1)}, bf16[192,2560]{1,0:T(8,128)(2,1)S(1)}, u32[]{:S(2)}, u32[]{:S(2)}) collective-permute-start(bf16[192,2560]{1,0:T(8,128)(2,1)} %copy-done.27), channel_id=1, source_target_pairs={{0,1},{1,0},{2,3},{3,2},{4,5},{5,4},{6,7},{7,6},{8,9},{9,8},{10,11... | collective-permute-start | bytes 2949128 | tf_op jit(solution)/shard_map/own_sum/ppermute | solution.py:289
  124.1 28.9 %copy-start.19 = (bf16[192,2560]{1,0:T(8,128)(2,1)S(1)}, bf16[192,2560]{1,0:T(8,128)(2,1)}, u32[]{:S(2)}) copy-start(bf16[192,2560]{1,0:T(8,128)(2,1)} %copy-done.18) | copy-start | bytes 2949124
  134.7 13.7 %collective-permute-start.21 = (bf16[96,2560]{1,0:T(8,128)(2,1)S(1)}, bf16[96,2560]{1,0:T(8,128)(2,1)S(1)}, u32[]{:S(2)}, u32[]{:S(2)}) collective-permute-start(bf16[96,2560]{1,0:T(8,128)(2,1)S(1)} %sum_right0.1), channel_id=1, source_target_pairs={{0,2},{1,3},{2,4},{3,5},{4,6},{5,7},{6,0},{7,1},{8,10},{9,11},{10,... | collective-permute-start | bytes 1474568 | tf_op jit(solution)/shard_map/to_right0/ppermute | solution.py:285
  139.6 13.4 %collective-permute-start.23 = (bf16[96,2560]{1,0:T(8,128)(2,1)S(1)}, bf16[96,2560]{1,0:T(8,128)(2,1)S(1)}, u32[]{:S(2)}, u32[]{:S(2)}) collective-permute-start(bf16[96,2560]{1,0:T(8,128)(2,1)S(1)} %sum_left1.1), channel_id=1, source_target_pairs={{0,6},{1,7},{2,0},{3,1},{4,2},{5,3},{6,4},{7,5},{8,14},{9,15},{10,... | collective-permute-start | bytes 1474568 | tf_op jit(solution)/shard_map/to_left1/ppermute | solution.py:285
  156.4 35.2 %all-to-all-start.2 = ((bf16[32,24,640]{2,1,0:T(8,128)(2,1)}), bf16[32,24,640]{2,1,0:T(8,128)(2,1)S(1)}, u32[]{:S(2)}, u32[]{:S(2)}) async-start(bf16[32,24,640]{2,1,0:T(8,128)(2,1)} %bitcast.13), calls=%async_computation.2 | async-start | bytes 1966080 | tf_op jit(solution)/shard_map/back/all_to_all | solution.py:255
  166.1 1.3 collective-permute-start.24
  167.3 3.8 %collective-permute-start.25 = (f32[1,2560]{1,0:T(1,128)S(1)}, f32[1,2560]{1,0:T(1,128)S(1)}, u32[]{:S(2)}, u32[]{:S(2)}) collective-permute-start(f32[1,2560]{1,0:T(1,128)S(1)} %add.47), channel_id=1, source_target_pairs={{0,2},{1,3},{2,0},{3,1},{4,6},{5,7},{6,4},{7,5},{8,10},{9,11},{10,... | collective-permute-start | bytes 30728 | tf_op jit(solution)/shard_map/ppermute | solution.py:333
  171.1 5.3 %collective-permute-start.26 = (f32[1,2560]{1,0:T(1,128)S(1)}, f32[1,2560]{1,0:T(1,128)S(1)}, u32[]{:S(2)}, u32[]{:S(2)}) collective-permute-start(f32[1,2560]{1,0:T(1,128)S(1)} %add.48), channel_id=1, source_target_pairs={{0,4},{1,5},{2,6},{3,7},{4,0},{5,1},{6,2},{7,3},{8,12},{9,13},{10,... | collective-permute-start | bytes 30728 | tf_op jit(solution)/shard_map/ppermute | solution.py:333
  192.3 15.7 %all-to-all-start.3 = ((bf16[32,4,640]{2,1,0:T(4,128)(2,1)}), bf16[32,4,640]{2,1,0:T(4,128)(2,1)S(1)}, u32[]{:S(2)}, u32[]{:S(2)}) async-start(bf16[32,4,640]{2,1,0:T(4,128)(2,1)} %broadcast_in_dim.8), calls=%async_computation.3 | async-start | bytes 327680 | tf_op jit(solution)/shard_map/all_to_all | solution.py:337
  (12 other events, 11.0 us)

commit v2 on v1

--- a/solution.py
+++ b/solution.py
@@ -126,9 +126,14 @@
             terms = dot(dg_ref[...], wg_ref[cols, :], NT) + dot(du_ref[...], wu_ref[cols, :], NT)
             out_ref[spot, cols] = terms.astype(BF16)
 
-        @pl.loop(0, width // COLUMNS)
-        def _(i):
-            tile(pl.multiple_of(i * COLUMNS, COLUMNS))
+        if first == HOPS.index(2):
+            for i in range(width // COLUMNS):
+                tile(i * COLUMNS)
+        else:
+
+            @pl.loop(0, width // COLUMNS)
+            def _(i):
+                tile(pl.multiple_of(i * COLUMNS, COLUMNS))
 
         for i in range(2 * j, 2 * j + 2):
             copy = pltpu.make_async_copy(out_ref.at[pl.ds(i * slots, slots)], outs[i], out_sem.at[i])

time: 210 us -> 209 us (level)
  transfers between devices with their start and end apart: 31 -> 31, of which waited for: 14 -> 14; matrix products, arithmetic and copies ran while one was open for 0% -> 0% of each run, Pallas kernels for 18% -> 17%
where the time goes in v2:
time: 209 us; the launch traced here: 208 us
  waiting for transfers between devices  90.7 us (43%)
  starting transfers between devices  50.7 us (24%)
  Pallas kernels  44.7 us (21%)
  local copies, waits for them, and re-layouts  19.9 us (10%)
    all_to_all x3, waiting for transfers between devices, exchange(): lax.all_to_all(shaped, axis, split_axis=0, concat_axis=0, tiled=True)  39.7 us
    ppermute x12, waiting for transfers between devices, shift(): lax.ppermute(x, 'etp', [(i, (i // 2 + by) % chips * 2 + i % 2) for i in r...  28.2 us
    all_to_all x3, starting transfers between devices, exchange(): lax.all_to_all(shaped, axis, split_axis=0, concat_axis=0, tiled=True)  26.7 us
    pallas_call x3, Pallas kernels, expert(): pl.pallas_call(functools.partial(expert_kernel, first, counts), in_specs=...  25.4 us
    unnamed x59, local copies, waits for them, and re-layouts  19 us
    ppermute x12, starting transfers between devices, shift(): lax.ppermute(x, 'etp', [(i, (i // 2 + by) % chips * 2 + i % 2) for i in r...  16 us
    ppermute x3, waiting for transfers between devices, local(): lax.ppermute(column, 'etp', [(i, i ^ bit) for i in range(n_etp)])  9.98 us
    all_to_all x1, waiting for transfers between devices, local(): lax.all_to_all(spread, 'expert', split_axis=0, concat_axis=0, tiled=True)  8.92 us
  transfers between devices with their start and end apart: 31, of which 14 were waited for; matrix products, arithmetic and copies ran while one was open for 0% of the time, Pallas kernels for 17%

profile of v2, /device:TPU:6, one launch (start us, length us, event | category | flops | bytes accessed | tf_op | source)
XLA Modules:
  0.0 207.8 jit_solution(7173849823000952681)
XLA Ops:
  1.6 1.1 copy-done.20
  3.4 2.3 %pack_grad.1 = bf16[768,640]{1,0:T(8,128)(2,1)} custom-call(s32[1,128]{1,0:T(1,128)S(1)} %bitcast.40, bf16[128,2560]{1,0:T(8,128)(2,1)S(1)} %copy-done.20), custom_call_target="tpu_custom_call" | custom-call | bytes 1048576 | tf_op jit(solution)/shard_map/pack_grad/pallas_call | solution.py:65
  5.7 11.6 %all-to-all-start = ((bf16[32,24,640]{2,1,0:T(8,128)(2,1)}), bf16[32,24,640]{2,1,0:T(8,128)(2,1)}, u32[]{:S(2)}, u32[]{:S(2)}) async-start(bf16[32,24,640]{2,1,0:T(8,128)(2,1)} %bitcast.4), calls=%async_computation | async-start | bytes 1966080 | tf_op jit(solution)/shard_map/grads/all_to_all | solution.py:260
  17.3 1.3 pack_tok.1
  18.6 1.0 copy-done.7
  19.6 24.5 %all-to-all-done = bf16[32,24,640]{2,1,0:T(8,128)(2,1)} async-done(((bf16[32,24,640]{2,1,0:T(8,128)(2,1)}), bf16[32,24,640]{2,1,0:T(8,128)(2,1)}, u32[]{:S(2)}, u32[]{:S(2)}) %all-to-all-start) | async-done | bytes 983072 | tf_op jit(solution)/shard_map/grads/all_to_all | solution.py:260
  44.2 3.1 %unpack_grad.1 = (bf16[96,2560]{1,0:T(8,128)(2,1)}, bf16[96,2560]{1,0:T(8,128)(2,1)}) custom-call(bf16[768,640]{1,0:T(8,128)(2,1)} %bitcast.5.packed_ref), custom_call_target="tpu_custom_call" | custom-call | bytes 1048576 | tf_op jit(solution)/shard_map/unpack_grad/pallas_call | solution.py:88
  47.7 0.8 collective-permute-start.8
  48.5 2.4 %collective-permute-start.3 = (bf16[96,2560]{1,0:T(8,128)(2,1)}, bf16[96,2560]{1,0:T(8,128)(2,1)}, u32[]{:S(2)}, u32[]{:S(2)}) collective-permute-start(bf16[96,2560]{1,0:T(8,128)(2,1)} %get-tuple-element.39.refs_0_), channel_id=1, source_target_pairs={{0,2},{1,3},{2,4},{3,5},{4,6},{5,7},{6,0},{7,1},{8,10},{9,11},{10,... | collective-permute-start | bytes 1474568 | tf_op jit(solution)/shard_map/left0/ppermute | solution.py:290
  51.0 0.8 copy-done.23
  51.8 3.2 %collective-permute-start.4 = (bf16[96,2560]{1,0:T(8,128)(2,1)}, bf16[96,2560]{1,0:T(8,128)(2,1)}, u32[]{:S(2)}, u32[]{:S(2)}) collective-permute-start(bf16[96,2560]{1,0:T(8,128)(2,1)} %get-tuple-element.40.refs_1_), channel_id=1, source_target_pairs={{0,2},{1,3},{2,4},{3,5},{4,6},{5,7},{6,0},{7,1},{8,10},{9,11},{10,... | collective-permute-start | bytes 1474568 | tf_op jit(solution)/shard_map/left1/ppermute | solution.py:290
  55.0 5.4 %all-to-all-start.1 = ((bf16[32,24,640]{2,1,0:T(8,128)(2,1)}), bf16[32,24,640]{2,1,0:T(8,128)(2,1)}, u32[]{:S(2)}, u32[]{:S(2)}) async-start(bf16[32,24,640]{2,1,0:T(8,128)(2,1)} %bitcast.38), calls=%async_computation.1 | async-start | bytes 1966080 | tf_op jit(solution)/shard_map/toks/all_to_all | solution.py:260
  60.5 1.7 copy-done.2
  62.2 1.7 copy-done.3
  64.0 1.4 copy-done.4
  65.4 1.4 copy-done.6
  66.8 1.0 copy-done.24
  67.8 7.1 %expert_own.1 = (bf16[192,2560]{1,0:T(8,128)(2,1)S(1)}, bf16[192,2560]{1,0:T(8,128)(2,1)S(1)}) custom-call(s32[8]{0:T(128)S(1)} %reshape.41.ids_ref, bf16[96,2560]{1,0:T(8,128)(2,1)} %get-tuple-element.39.refs_0_, bf16[96,2560]{1,0:T(8,128)(2,1)} %get-tuple-element.40.refs_1_, bf16[96,2560]{1,0:T(8,128)(2,1)S(1)} %copy-done.24, ...), custom_call_target="tpu_custom_call" | custom-call | bytes 1048576 | tf_op jit(solution)/shard_map/expert_own/pallas_call | solution.py:155
  74.9 1.0 copy-done.18
  75.8 1.0 copy-done.27
  77.9 2.4 %collective-permute-done.9.refs_6_ = bf16[96,2560]{1,0:T(8,128)(2,1)S(1)} collective-permute-done((bf16[96,2560]{1,0:T(8,128)(2,1)}, bf16[96,2560]{1,0:T(8,128)(2,1)S(1)}, u32[]{:S(2)}, u32[]{:S(2)}) %collective-permute-start.9) | collective-permute-done | bytes 491552 | tf_op jit(solution)/shard_map/right_x0/ppermute | solution.py:294
  81.0 12.4 %expert_sides.1 = (bf16[192,2560]{1,0:T(8,128)(2,1)S(1)}, bf16[192,2560]{1,0:T(8,128)(2,1)S(1)}, bf16[192,2560]{1,0:T(8,128)(2,1)S(1)}, bf16[192,2560]{1,0:T(8,128)(2,1)S(1)}) custom-call(s32[8]{0:T(128)S(1)} %reshape.41.ids_ref, bf16[96,2560]{1,0:T(8,128)(2,1)} %collective-permute-done.3.refs_0_, bf16[96,2560]{1,0:T(8,128)(2,1)} %collective-permute-done.4.refs_1_, ...), custom_call_target="tpu_custom_call" | custom-call | bytes 1048576 | tf_op jit(solution)/shard_map/expert_sides/pallas_call | solution.py:155
  94.0 0.8 collective-permute-done.14.refs_1_
  97.0 0.9 copy-done.8
  99.0 0.8 copy-done.22
  99.8 5.9 %expert_far.1 = (bf16[192,2560]{1,0:T(8,128)(2,1)S(1)}, bf16[192,2560]{1,0:T(8,128)(2,1)S(1)}) custom-call(s32[8]{0:T(128)S(1)} %reshape.41.ids_ref, bf16[96,2560]{1,0:T(8,128)(2,1)S(1)} %collective-permute-done.11.refs_0_, bf16[96,2560]{1,0:T(8,128)(2,1)S(1)} %collective-permute-done.14.refs_1_, bf16[96,2560]{1,0:T(8,128)(2,1)S(1)} %collective-permute-done.15.refs_2_, ...), custom_call_target="tpu_custom_call" | custom-call | bytes 1048576 | tf_op jit(solution)/shard_map/expert_far/pallas_call | solution.py:155
  105.8 1.0 copy-done.16
  106.7 1.0 copy-done.28
  107.9 3.2 %collective-permute-start.19 = (bf16[96,2560]{1,0:T(8,128)(2,1)}, bf16[96,2560]{1,0:T(8,128)(2,1)S(1)}, u32[]{:S(2)}, u32[]{:S(2)}) collective-permute-start(bf16[96,2560]{1,0:T(8,128)(2,1)} %copy-done.22), channel_id=1, source_target_pairs={{0,2},{1,3},{2,4},{3,5},{4,6},{5,7},{6,0},{7,1},{8,10},{9,11},{10,... | collective-permute-start | bytes 1474568 | tf_op jit(solution)/shard_map/to_right1/ppermute | solution.py:290
  111.1 1.2 copy-done.17
  113.1 2.2 %collective-permute-start.20 = (bf16[96,2560]{1,0:T(8,128)(2,1)S(1)}, bf16[96,2560]{1,0:T(8,128)(2,1)S(1)}, u32[]{:S(2)}, u32[]{:S(2)}) collective-permute-start(bf16[96,2560]{1,0:T(8,128)(2,1)S(1)} %sum_far0.1), channel_id=1, source_target_pairs={{0,2},{1,3},{2,4},{3,5},{4,6},{5,7},{6,0},{7,1},{8,10},{9,11},{10,... | collective-permute-start | bytes 1474568 | tf_op jit(solution)/shard_map/via_right/ppermute | solution.py:290
  116.3 2.2 %unpack_tok.1 = (bf16[96,2560]{1,0:T(8,128)(2,1)S(1)}, bf16[96,2560]{1,0:T(8,128)(2,1)S(1)}) custom-call(bf16[768,640]{1,0:T(8,128)(2,1)} %bitcast.12.packed_ref), custom_call_target="tpu_custom_call" | custom-call | bytes 1048576 | tf_op jit(solution)/shard_map/unpack_tok/pallas_call | solution.py:88
  118.4 4.7 %collective-permute-done.18.refs_1_ = bf16[96,2560]{1,0:T(8,128)(2,1)S(1)} collective-permute-done((bf16[96,2560]{1,0:T(8,128)(2,1)S(1)}, bf16[96,2560]{1,0:T(8,128)(2,1)S(1)}, u32[]{:S(2)}, u32[]{:S(2)}) %collective-permute-start.18) | collective-permute-done | bytes 491552 | tf_op jit(solution)/shard_map/to_left0/ppermute | solution.py:290
  123.1 9.4 %collective-permute-done.20.refs_2_ = bf16[96,2560]{1,0:T(8,128)(2,1)S(1)} collective-permute-done((bf16[96,2560]{1,0:T(8,128)(2,1)S(1)}, bf16[96,2560]{1,0:T(8,128)(2,1)S(1)}, u32[]{:S(2)}, u32[]{:S(2)}) %collective-permute-start.20) | collective-permute-done | bytes 491552 | tf_op jit(solution)/shard_map/via_right/ppermute | solution.py:290
  132.6 1.1 sum_right0.1
  133.7 3.8 %collective-permute-start.21 = (bf16[96,2560]{1,0:T(8,128)(2,1)S(1)}, bf16[96,2560]{1,0:T(8,128)(2,1)S(1)}, u32[]{:S(2)}, u32[]{:S(2)}) collective-permute-start(bf16[96,2560]{1,0:T(8,128)(2,1)S(1)} %sum_right0.1), channel_id=1, source_target_pairs={{0,2},{1,3},{2,4},{3,5},{4,6},{5,7},{6,0},{7,1},{8,10},{9,11},{10,... | collective-permute-start | bytes 1474568 | tf_op jit(solution)/shard_map/to_right0/ppermute | solution.py:290
  137.5 1.1 sum_left1.1
  138.8 8.6 %collective-permute-done.21.refs_0_ = bf16[96,2560]{1,0:T(8,128)(2,1)S(1)} collective-permute-done((bf16[96,2560]{1,0:T(8,128)(2,1)S(1)}, bf16[96,2560]{1,0:T(8,128)(2,1)S(1)}, u32[]{:S(2)}, u32[]{:S(2)}) %collective-permute-start.21) | collective-permute-done | bytes 491552 | tf_op jit(solution)/shard_map/to_right0/ppermute | solution.py:290
  147.4 4.7 %collective-permute-done.23.refs_3_ = bf16[96,2560]{1,0:T(8,128)(2,1)S(1)} collective-permute-done((bf16[96,2560]{1,0:T(8,128)(2,1)S(1)}, bf16[96,2560]{1,0:T(8,128)(2,1)S(1)}, u32[]{:S(2)}, u32[]{:S(2)}) %collective-permute-start.23) | collective-permute-done | bytes 491552 | tf_op jit(solution)/shard_map/to_left1/ppermute | solution.py:290
  152.0 3.3 %token_math.1 = (bf16[768,640]{1,0:T(8,128)(2,1)}, f32[1,2560]{1,0:T(1,128)S(1)}) custom-call(bf16[1,2560]{1,0:T(2,128)(2,1)S(1)} %dynamic-slice_bitcast_fusion.router_ref, bf16[192,2560]{1,0:T(8,128)(2,1)S(1)} %copy-done.19, bf16[192,2560]{1,0:T(8,128)(2,1)S(1)} %collective-permute-done.2.keep_r_ref, bf16[96,2560]{1,0:T(8,128)(2,1)S(1)} %collective-permute-done.21.refs_0_, ...), custom_call_target="tpu_custom_call" | custom-call | bytes 1048576 | tf_op jit(solution)/shard_map/token_math/pallas_call | solution.py:226
  155.4 9.7 %all-to-all-start.2 = ((bf16[32,24,640]{2,1,0:T(8,128)(2,1)}), bf16[32,24,640]{2,1,0:T(8,128)(2,1)S(1)}, u32[]{:S(2)}, u32[]{:S(2)}) async-start(bf16[32,24,640]{2,1,0:T(8,128)(2,1)} %bitcast.13), calls=%async_computation.2 | async-start | bytes 1966080 | tf_op jit(solution)/shard_map/back/all_to_all | solution.py:260
  165.2 1.2 collective-permute-done.24
  166.5 3.7 %collective-permute-done.25 = f32[1,2560]{1,0:T(1,128)S(1)} collective-permute-done((f32[1,2560]{1,0:T(1,128)S(1)}, f32[1,2560]{1,0:T(1,128)S(1)}, u32[]{:S(2)}, u32[]{:S(2)}) %collective-permute-start.25) | collective-permute-done | bytes 10272 | tf_op jit(solution)/shard_map/ppermute | solution.py:338
  170.3 5.2 %collective-permute-done.26 = f32[1,2560]{1,0:T(1,128)S(1)} collective-permute-done((f32[1,2560]{1,0:T(1,128)S(1)}, f32[1,2560]{1,0:T(1,128)S(1)}, u32[]{:S(2)}, u32[]{:S(2)}) %collective-permute-start.26) | collective-permute-done | bytes 10272 | tf_op jit(solution)/shard_map/ppermute | solution.py:338
  175.4 15.1 %all-to-all-done.2 = bf16[32,24,640]{2,1,0:T(8,128)(2,1)S(1)} async-done(((bf16[32,24,640]{2,1,0:T(8,128)(2,1)}), bf16[32,24,640]{2,1,0:T(8,128)(2,1)S(1)}, u32[]{:S(2)}, u32[]{:S(2)}) %all-to-all-start.2) | async-done | bytes 983072 | tf_op jit(solution)/shard_map/back/all_to_all | solution.py:260
  191.3 4.9 %all-to-all-start.3 = ((bf16[32,4,640]{2,1,0:T(4,128)(2,1)}), bf16[32,4,640]{2,1,0:T(4,128)(2,1)S(1)}, u32[]{:S(2)}, u32[]{:S(2)}) async-start(bf16[32,4,640]{2,1,0:T(4,128)(2,1)} %broadcast_in_dim.8), calls=%async_computation.3 | async-start | bytes 327680 | tf_op jit(solution)/shard_map/all_to_all | solution.py:342
  196.3 1.8 final.1
  198.1 8.9 %all-to-all-done.3 = bf16[32,4,640]{2,1,0:T(4,128)(2,1)S(1)} async-done(((bf16[32,4,640]{2,1,0:T(4,128)(2,1)}), bf16[32,4,640]{2,1,0:T(4,128)(2,1)S(1)}, u32[]{:S(2)}, u32[]{:S(2)}) %all-to-all-start.3) | async-done | bytes 163872 | tf_op jit(solution)/shard_map/all_to_all | solution.py:342
  (100 shorter events, 11.6 us)
Async XLA Ops:
  0.6 16.6 %copy-start.26 = (s32[128,1]{0,1:T(1,128)S(1)}, s32[128,1]{0,1:T(1,128)}, u32[]{:S(2)}) copy-start(s32[128,1]{0,1:T(1,128)} %param.13) | copy-start | bytes 1540
  1.6 1.1 copy-start.20
  3.4 13.9 %copy-start.21 = (bf16[128,2560]{1,0:T(8,128)(2,1)S(1)}, bf16[128,2560]{1,0:T(8,128)(2,1)}, u32[]{:S(2)}) copy-start(bf16[128,2560]{1,0:T(8,128)(2,1)} %rows_ref.2) | copy-start | bytes 1966084
  5.7 38.5 %all-to-all-start = ((bf16[32,24,640]{2,1,0:T(8,128)(2,1)}), bf16[32,24,640]{2,1,0:T(8,128)(2,1)}, u32[]{:S(2)}, u32[]{:S(2)}) async-start(bf16[32,24,640]{2,1,0:T(8,128)(2,1)} %bitcast.4), calls=%async_computation | async-start | bytes 1966080 | tf_op jit(solution)/shard_map/grads/all_to_all | solution.py:260
  17.3 43.2 %copy-start.1 = (bf16[1,512,2560]{2,1,0:T(8,128)(2,1)S(1)}, bf16[1,512,2560]{2,1,0:T(8,128)(2,1)}, u32[]{:S(2)}) copy-start(bf16[1,512,2560]{2,1,0:T(8,128)(2,1)} %param.18) | copy-start | bytes 7864324
  47.2 3.8 %collective-permute-start = (bf16[96,2560]{1,0:T(8,128)(2,1)}, bf16[96,2560]{1,0:T(8,128)(2,1)S(1)}, u32[]{:S(2)}, u32[]{:S(2)}) collective-permute-start(bf16[96,2560]{1,0:T(8,128)(2,1)} %get-tuple-element.39.refs_0_), channel_id=1, source_target_pairs={{0,1},{1,0},{2,3},{3,2},{4,5},{5,4},{6,7},{7,6},{8,9},{9,8},{10,11... | collective-permute-start | bytes 1474568 | tf_op jit(solution)/shard_map/own_x0/ppermute | solution.py:294
  47.2 13.2 %collective-permute-start.1 = (bf16[96,2560]{1,0:T(8,128)(2,1)}, bf16[96,2560]{1,0:T(8,128)(2,1)}, u32[]{:S(2)}, u32[]{:S(2)}) collective-permute-start(bf16[96,2560]{1,0:T(8,128)(2,1)} %get-tuple-element.40.refs_1_), channel_id=1, source_target_pairs={{0,1},{1,0},{2,3},{3,2},{4,5},{5,4},{6,7},{7,6},{8,9},{9,8},{10,11... | collective-permute-start | bytes 1474568 | tf_op jit(solution)/shard_map/own_x1/ppermute | solution.py:294
  47.7 29.1 %collective-permute-start.8 = (bf16[96,2560]{1,0:T(8,128)(2,1)}, bf16[96,2560]{1,0:T(8,128)(2,1)S(1)}, u32[]{:S(2)}, u32[]{:S(2)}) collective-permute-start(bf16[96,2560]{1,0:T(8,128)(2,1)} %get-tuple-element.40.refs_1_), channel_id=1, source_target_pairs={{0,6},{1,7},{2,0},{3,1},{4,2},{5,3},{6,4},{7,5},{8,14},{9,15},{10,... | collective-permute-start | bytes 1474568 | tf_op jit(solution)/shard_map/right1/ppermute | solution.py:290
  48.5 28.3 %collective-permute-start.3 = (bf16[96,2560]{1,0:T(8,128)(2,1)}, bf16[96,2560]{1,0:T(8,128)(2,1)}, u32[]{:S(2)}, u32[]{:S(2)}) collective-permute-start(bf16[96,2560]{1,0:T(8,128)(2,1)} %get-tuple-element.39.refs_0_), channel_id=1, source_target_pairs={{0,2},{1,3},{2,4},{3,5},{4,6},{5,7},{6,0},{7,1},{8,10},{9,11},{10,... | collective-permute-start | bytes 1474568 | tf_op jit(solution)/shard_map/left0/ppermute | solution.py:290
  51.0 25.9 %collective-permute-start.7 = (bf16[96,2560]{1,0:T(8,128)(2,1)}, bf16[96,2560]{1,0:T(8,128)(2,1)}, u32[]{:S(2)}, u32[]{:S(2)}) collective-permute-start(bf16[96,2560]{1,0:T(8,128)(2,1)} %get-tuple-element.39.refs_0_), channel_id=1, source_target_pairs={{0,6},{1,7},{2,0},{3,1},{4,2},{5,3},{6,4},{7,5},{8,14},{9,15},{10,... | collective-permute-start | bytes 1474568 | tf_op jit(solution)/shard_map/right0/ppermute | solution.py:290
  51.8 25.6 %collective-permute-start.4 = (bf16[96,2560]{1,0:T(8,128)(2,1)}, bf16[96,2560]{1,0:T(8,128)(2,1)}, u32[]{:S(2)}, u32[]{:S(2)}) collective-permute-start(bf16[96,2560]{1,0:T(8,128)(2,1)} %get-tuple-element.40.refs_1_), channel_id=1, source_target_pairs={{0,2},{1,3},{2,4},{3,5},{4,6},{5,7},{6,0},{7,1},{8,10},{9,11},{10,... | collective-permute-start | bytes 1474568 | tf_op jit(solution)/shard_map/left1/ppermute | solution.py:290
  55.0 52.7 %all-to-all-start.1 = ((bf16[32,24,640]{2,1,0:T(8,128)(2,1)}), bf16[32,24,640]{2,1,0:T(8,128)(2,1)}, u32[]{:S(2)}, u32[]{:S(2)}) async-start(bf16[32,24,640]{2,1,0:T(8,128)(2,1)} %bitcast.38), calls=%async_computation.1 | async-start | bytes 1966080 | tf_op jit(solution)/shard_map/toks/all_to_all | solution.py:260
  60.5 1.7 copy-start.2
  62.2 1.7 copy-start.3
  64.0 1.4 copy-start.4
  65.4 1.4 copy-start.6
  67.8 13.2 %copy-start.5 = (bf16[1,1536,512]{2,1,0:T(8,128)(2,1)S(1)}, bf16[1,1536,512]{2,1,0:T(8,128)(2,1)}, u32[]{:S(2)}) copy-start(bf16[1,1536,512]{2,1,0:T(8,128)(2,1)} %param.14) | copy-start | bytes 4718596
  76.8 4.2 %collective-permute-start.5 = (bf16[96,2560]{1,0:T(8,128)(2,1)}, bf16[96,2560]{1,0:T(8,128)(2,1)S(1)}, u32[]{:S(2)}, u32[]{:S(2)}) collective-permute-start(bf16[96,2560]{1,0:T(8,128)(2,1)} %collective-permute-done.3.refs_0_), channel_id=1, source_target_pairs={{0,1},{1,0},{2,3},{3,2},{4,5},{5,4},{6,7},{7,6},{8,9},{9,8},{10,11... | collective-permute-start | bytes 1474568 | tf_op jit(solution)/shard_map/left_x0/ppermute | solution.py:294
  76.8 3.5 %collective-permute-start.9 = (bf16[96,2560]{1,0:T(8,128)(2,1)}, bf16[96,2560]{1,0:T(8,128)(2,1)S(1)}, u32[]{:S(2)}, u32[]{:S(2)}) collective-permute-start(bf16[96,2560]{1,0:T(8,128)(2,1)} %collective-permute-done.7.refs_4_), channel_id=1, source_target_pairs={{0,1},{1,0},{2,3},{3,2},{4,5},{5,4},{6,7},{7,6},{8,9},{9,8},{10,11... | collective-permute-start | bytes 1474568 | tf_op jit(solution)/shard_map/right_x0/ppermute | solution.py:294
  77.3 3.7 %collective-permute-start.6 = (bf16[96,2560]{1,0:T(8,128)(2,1)}, bf16[96,2560]{1,0:T(8,128)(2,1)S(1)}, u32[]{:S(2)}, u32[]{:S(2)}) collective-permute-start(bf16[96,2560]{1,0:T(8,128)(2,1)} %collective-permute-done.4.refs_1_), channel_id=1, source_target_pairs={{0,1},{1,0},{2,3},{3,2},{4,5},{5,4},{6,7},{7,6},{8,9},{9,8},{10,11... | collective-permute-start | bytes 1474568 | tf_op jit(solution)/shard_map/left_x1/ppermute | solution.py:294
  77.4 3.6 %collective-permute-start.10 = (bf16[96,2560]{1,0:T(8,128)(2,1)S(1)}, bf16[96,2560]{1,0:T(8,128)(2,1)S(1)}, u32[]{:S(2)}, u32[]{:S(2)}) collective-permute-start(bf16[96,2560]{1,0:T(8,128)(2,1)S(1)} %collective-permute-done.8.refs_5_), channel_id=1, source_target_pairs={{0,1},{1,0},{2,3},{3,2},{4,5},{5,4},{6,7},{7,6},{8,9},{9,8},{10,11... | collective-permute-start | bytes 1474568 | tf_op jit(solution)/shard_map/right_x1/ppermute | solution.py:294
  77.8 16.9 %collective-permute-start.11 = (bf16[96,2560]{1,0:T(8,128)(2,1)}, bf16[96,2560]{1,0:T(8,128)(2,1)S(1)}, u32[]{:S(2)}, u32[]{:S(2)}) collective-permute-start(bf16[96,2560]{1,0:T(8,128)(2,1)} %collective-permute-done.3.refs_0_), channel_id=1, source_target_pairs={{0,2},{1,3},{2,4},{3,5},{4,6},{5,7},{6,0},{7,1},{8,10},{9,11},{10,... | collective-permute-start | bytes 1474568 | tf_op jit(solution)/shard_map/far0/ppermute | solution.py:290
  80.3 14.5 %collective-permute-start.14 = (bf16[96,2560]{1,0:T(8,128)(2,1)S(1)}, bf16[96,2560]{1,0:T(8,128)(2,1)S(1)}, u32[]{:S(2)}, u32[]{:S(2)}) collective-permute-start(bf16[96,2560]{1,0:T(8,128)(2,1)S(1)} %collective-permute-done.8.refs_5_), channel_id=1, source_target_pairs={{0,6},{1,7},{2,0},{3,1},{4,2},{5,3},{6,4},{7,5},{8,14},{9,15},{10,... | collective-permute-start | bytes 1474568 | tf_op jit(solution)/shard_map/far1/ppermute | solution.py:290
  93.4 4.6 %copy-start.12 = (bf16[192,2560]{1,0:T(8,128)(2,1)}, bf16[192,2560]{1,0:T(8,128)(2,1)S(1)}, u32[]{:S(2)}) copy-start(bf16[192,2560]{1,0:T(8,128)(2,1)S(1)} %get-tuple-element.58.refs_0_) | copy-start | bytes 2949124
  93.4 2.7 %collective-permute-start.12 = (bf16[192,2560]{1,0:T(8,128)(2,1)S(1)}, bf16[192,2560]{1,0:T(8,128)(2,1)S(1)}, u32[]{:S(2)}, u32[]{:S(2)}) collective-permute-start(bf16[192,2560]{1,0:T(8,128)(2,1)S(1)} %get-tuple-element.49), channel_id=1, source_target_pairs={{0,1},{1,0},{2,3},{3,2},{4,5},{5,4},{6,7},{7,6},{8,9},{9,8},{10,11... | collective-permute-start | bytes 2949128 | tf_op jit(solution)/shard_map/left_sum/ppermute | solution.py:294
  93.6 4.3 %collective-permute-start.13 = (bf16[192,2560]{1,0:T(8,128)(2,1)S(1)}, bf16[192,2560]{1,0:T(8,128)(2,1)S(1)}, u32[]{:S(2)}, u32[]{:S(2)}) collective-permute-start(bf16[192,2560]{1,0:T(8,128)(2,1)S(1)} %get-tuple-element.50), channel_id=1, source_target_pairs={{0,1},{1,0},{2,3},{3,2},{4,5},{5,4},{6,7},{7,6},{8,9},{9,8},{10,11... | collective-permute-start | bytes 2949128 | tf_op jit(solution)/shard_map/right_sum/ppermute | solution.py:294
  94.8 5.0 %collective-permute-start.15 = (bf16[96,2560]{1,0:T(8,128)(2,1)S(1)}, bf16[96,2560]{1,0:T(8,128)(2,1)S(1)}, u32[]{:S(2)}, u32[]{:S(2)}) collective-permute-start(bf16[96,2560]{1,0:T(8,128)(2,1)S(1)} %collective-permute-done.11.refs_0_), channel_id=1, source_target_pairs={{0,1},{1,0},{2,3},{3,2},{4,5},{5,4},{6,7},{7,6},{8,9},{9,8},{10,11... | collective-permute-start | bytes 1474568 | tf_op jit(solution)/shard_map/far_x0/ppermute | solution.py:294
  94.8 5.0 %collective-permute-start.16 = (bf16[96,2560]{1,0:T(8,128)(2,1)S(1)}, bf16[96,2560]{1,0:T(8,128)(2,1)S(1)}, u32[]{:S(2)}, u32[]{:S(2)}) collective-permute-start(bf16[96,2560]{1,0:T(8,128)(2,1)S(1)} %collective-permute-done.14.refs_1_), channel_id=1, source_target_pairs={{0,1},{1,0},{2,3},{3,2},{4,5},{5,4},{6,7},{7,6},{8,9},{9,8},{10,11... | collective-permute-start | bytes 1474568 | tf_op jit(solution)/shard_map/far_x1/ppermute | solution.py:294
  98.0 1.1 copy-start.14
  107.7 3.4 %collective-permute-start.17 = (bf16[192,2560]{1,0:T(8,128)(2,1)}, bf16[192,2560]{1,0:T(8,128)(2,1)S(1)}, u32[]{:S(2)}, u32[]{:S(2)}) collective-permute-start(bf16[192,2560]{1,0:T(8,128)(2,1)} %copy-done.28), channel_id=1, source_target_pairs={{0,1},{1,0},{2,3},{3,2},{4,5},{5,4},{6,7},{7,6},{8,9},{9,8},{10,11... | collective-permute-start | bytes 2949128 | tf_op jit(solution)/shard_map/far_sum/ppermute | solution.py:294
  107.9 15.3 %collective-permute-start.18 = (bf16[96,2560]{1,0:T(8,128)(2,1)S(1)}, bf16[96,2560]{1,0:T(8,128)(2,1)S(1)}, u32[]{:S(2)}, u32[]{:S(2)}) collective-permute-start(bf16[96,2560]{1,0:T(8,128)(2,1)S(1)} %sum_left0.1), channel_id=1, source_target_pairs={{0,6},{1,7},{2,0},{3,1},{4,2},{5,3},{6,4},{7,5},{8,14},{9,15},{10,... | collective-permute-start | bytes 1474568 | tf_op jit(solution)/shard_map/to_left0/ppermute | solution.py:290
  107.9 15.3 %collective-permute-start.19 = (bf16[96,2560]{1,0:T(8,128)(2,1)}, bf16[96,2560]{1,0:T(8,128)(2,1)S(1)}, u32[]{:S(2)}, u32[]{:S(2)}) collective-permute-start(bf16[96,2560]{1,0:T(8,128)(2,1)} %copy-done.22), channel_id=1, source_target_pairs={{0,2},{1,3},{2,4},{3,5},{4,6},{5,7},{6,0},{7,1},{8,10},{9,11},{10,... | collective-permute-start | bytes 1474568 | tf_op jit(solution)/shard_map/to_right1/ppermute | solution.py:290
  111.1 1.2 copy-start.17
  112.3 20.3 %copy-start.13 = (bf16[192,2560]{1,0:T(8,128)(2,1)S(1)}, bf16[192,2560]{1,0:T(8,128)(2,1)}, u32[]{:S(2)}) copy-start(bf16[192,2560]{1,0:T(8,128)(2,1)} %copy-done.12) | copy-start | bytes 2949124
  112.3 20.3 %copy-start.15 = (bf16[192,2560]{1,0:T(8,128)(2,1)S(1)}, bf16[192,2560]{1,0:T(8,128)(2,1)}, u32[]{:S(2)}) copy-start(bf16[192,2560]{1,0:T(8,128)(2,1)} %copy-done.14) | copy-start | bytes 2949124
  113.1 24.4 %copy-start.9 = (bf16[192,2560]{1,0:T(8,128)(2,1)S(1)}, bf16[192,2560]{1,0:T(8,128)(2,1)}, u32[]{:S(2)}) copy-start(bf16[192,2560]{1,0:T(8,128)(2,1)} %copy-done.8) | copy-start | bytes 2949124
  113.1 24.4 %copy-start.11 = (bf16[192,2560]{1,0:T(8,128)(2,1)S(1)}, bf16[192,2560]{1,0:T(8,128)(2,1)}, u32[]{:S(2)}) copy-start(bf16[192,2560]{1,0:T(8,128)(2,1)} %copy-done.10) | copy-start | bytes 2949124
  113.1 19.5 %collective-permute-start.20 = (bf16[96,2560]{1,0:T(8,128)(2,1)S(1)}, bf16[96,2560]{1,0:T(8,128)(2,1)S(1)}, u32[]{:S(2)}, u32[]{:S(2)}) collective-permute-start(bf16[96,2560]{1,0:T(8,128)(2,1)S(1)} %sum_far0.1), channel_id=1, source_target_pairs={{0,2},{1,3},{2,4},{3,5},{4,6},{5,7},{6,0},{7,1},{8,10},{9,11},{10,... | collective-permute-start | bytes 1474568 | tf_op jit(solution)/shard_map/via_right/ppermute | solution.py:290
  116.1 21.4 %collective-permute-start.22 = (bf16[96,2560]{1,0:T(8,128)(2,1)S(1)}, bf16[96,2560]{1,0:T(8,128)(2,1)S(1)}, u32[]{:S(2)}, u32[]{:S(2)}) collective-permute-start(bf16[96,2560]{1,0:T(8,128)(2,1)S(1)} %sum_far1.1), channel_id=1, source_target_pairs={{0,6},{1,7},{2,0},{3,1},{4,2},{5,3},{6,4},{7,5},{8,14},{9,15},{10,... | collective-permute-start | bytes 1474568 | tf_op jit(solution)/shard_map/via_left/ppermute | solution.py:290
  116.3 22.5 %collective-permute-start.2 = (bf16[192,2560]{1,0:T(8,128)(2,1)}, bf16[192,2560]{1,0:T(8,128)(2,1)S(1)}, u32[]{:S(2)}, u32[]{:S(2)}) collective-permute-start(bf16[192,2560]{1,0:T(8,128)(2,1)} %copy-done.27), channel_id=1, source_target_pairs={{0,1},{1,0},{2,3},{3,2},{4,5},{5,4},{6,7},{7,6},{8,9},{9,8},{10,11... | collective-permute-start | bytes 2949128 | tf_op jit(solution)/shard_map/own_sum/ppermute | solution.py:294
  123.1 28.9 %copy-start.19 = (bf16[192,2560]{1,0:T(8,128)(2,1)S(1)}, bf16[192,2560]{1,0:T(8,128)(2,1)}, u32[]{:S(2)}) copy-start(bf16[192,2560]{1,0:T(8,128)(2,1)} %copy-done.18) | copy-start | bytes 2949124
  133.7 13.7 %collective-permute-start.21 = (bf16[96,2560]{1,0:T(8,128)(2,1)S(1)}, bf16[96,2560]{1,0:T(8,128)(2,1)S(1)}, u32[]{:S(2)}, u32[]{:S(2)}) collective-permute-start(bf16[96,2560]{1,0:T(8,128)(2,1)S(1)} %sum_right0.1), channel_id=1, source_target_pairs={{0,2},{1,3},{2,4},{3,5},{4,6},{5,7},{6,0},{7,1},{8,10},{9,11},{10,... | collective-permute-start | bytes 1474568 | tf_op jit(solution)/shard_map/to_right0/ppermute | solution.py:290
  138.7 13.4 %collective-permute-start.23 = (bf16[96,2560]{1,0:T(8,128)(2,1)S(1)}, bf16[96,2560]{1,0:T(8,128)(2,1)S(1)}, u32[]{:S(2)}, u32[]{:S(2)}) collective-permute-start(bf16[96,2560]{1,0:T(8,128)(2,1)S(1)} %sum_left1.1), channel_id=1, source_target_pairs={{0,6},{1,7},{2,0},{3,1},{4,2},{5,3},{6,4},{7,5},{8,14},{9,15},{10,... | collective-permute-start | bytes 1474568 | tf_op jit(solution)/shard_map/to_left1/ppermute | solution.py:290
  155.4 35.2 %all-to-all-start.2 = ((bf16[32,24,640]{2,1,0:T(8,128)(2,1)}), bf16[32,24,640]{2,1,0:T(8,128)(2,1)S(1)}, u32[]{:S(2)}, u32[]{:S(2)}) async-start(bf16[32,24,640]{2,1,0:T(8,128)(2,1)} %bitcast.13), calls=%async_computation.2 | async-start | bytes 1966080 | tf_op jit(solution)/shard_map/back/all_to_all | solution.py:260
  165.1 1.3 collective-permute-start.24
  166.4 3.8 %collective-permute-start.25 = (f32[1,2560]{1,0:T(1,128)S(1)}, f32[1,2560]{1,0:T(1,128)S(1)}, u32[]{:S(2)}, u32[]{:S(2)}) collective-permute-start(f32[1,2560]{1,0:T(1,128)S(1)} %add.47), channel_id=1, source_target_pairs={{0,2},{1,3},{2,0},{3,1},{4,6},{5,7},{6,4},{7,5},{8,10},{9,11},{10,... | collective-permute-start | bytes 30728 | tf_op jit(solution)/shard_map/ppermute | solution.py:338
  170.2 5.3 %collective-permute-start.26 = (f32[1,2560]{1,0:T(1,128)S(1)}, f32[1,2560]{1,0:T(1,128)S(1)}, u32[]{:S(2)}, u32[]{:S(2)}) collective-permute-start(f32[1,2560]{1,0:T(1,128)S(1)} %add.48), channel_id=1, source_target_pairs={{0,4},{1,5},{2,6},{3,7},{4,0},{5,1},{6,2},{7,3},{8,12},{9,13},{10,... | collective-permute-start | bytes 30728 | tf_op jit(solution)/shard_map/ppermute | solution.py:338
  191.3 15.7 %all-to-all-start.3 = ((bf16[32,4,640]{2,1,0:T(4,128)(2,1)}), bf16[32,4,640]{2,1,0:T(4,128)(2,1)S(1)}, u32[]{:S(2)}, u32[]{:S(2)}) async-start(bf16[32,4,640]{2,1,0:T(4,128)(2,1)} %broadcast_in_dim.8), calls=%async_computation.3 | async-start | bytes 327680 | tf_op jit(solution)/shard_map/all_to_all | solution.py:342
  (12 other events, 11.0 us)

commit v3 on v2

--- a/solution.py
+++ b/solution.py
@@ -18,6 +18,7 @@
 BF16 = jnp.bfloat16
 PARAMS = pltpu.CompilerParams(vmem_limit_bytes=24 * 2**20)
 COLUMNS = 512
+EARLY = ("sum_left0", "sum_right1")
 HOPS = (0, -1, 1, 2)
 COST = pl.CostEstimate(flops=0, transcendentals=0, bytes_accessed=2**20)
 
@@ -186,7 +187,7 @@
         in_specs=[pl.BlockSpec(memory_space=pl.ANY)] * len(parts),
         out_shape=jax.ShapeDtypeStruct((rows, width), BF16),
         scratch_shapes=[pltpu.VMEM((rows, width), BF16)] * len(parts) + [pltpu.SemaphoreType.DMA((len(parts),))],
-        compiler_params=pltpu.CompilerParams(vmem_limit_bytes=12 * 2**20),
+        compiler_params=pltpu.CompilerParams(vmem_limit_bytes=(12 if name in EARLY else 56) * 2**20),
         cost_estimate=COST,
         name=name,
     )(*[part for part, _ in parts])

time: 209 us -> 213 us (1.019)
  Pallas kernels: 44.7 us -> 49.6 us
    pallas_call x6, Pallas kernels: 5.31 us -> 10.3 us  [add(): pl.pallas_call(functools.partial(add_kernel, tuple((start for _, start in...]
    unnamed x59 -> x57, local copies, waits for them, and re-layouts: 19 us -> 20.3 us
  transfers between devices with their start and end apart: 31 -> 31, of which waited for: 14 -> 15; matrix products, arithmetic and copies ran while one was open for 0% -> 0% of each run, Pallas kernels for 17% -> 19%
where the time goes in v3:
time: 213 us; the launch traced here: 212 us
  waiting for transfers between devices  88.7 us (42%)
  starting transfers between devices  50.6 us (24%)
  Pallas kernels  49.6 us (23%)
  local copies, waits for them, and re-layouts  21.2 us (10%)
    all_to_all x3, waiting for transfers between devices, exchange(): lax.all_to_all(shaped, axis, split_axis=0, concat_axis=0, tiled=True)  39.7 us
    all_to_all x3, starting transfers between devices, exchange(): lax.all_to_all(shaped, axis, split_axis=0, concat_axis=0, tiled=True)  26.7 us
    ppermute x12, waiting for transfers between devices, shift(): lax.ppermute(x, 'etp', [(i, (i // 2 + by) % chips * 2 + i % 2) for i in r...  26.1 us
    pallas_call x3, Pallas kernels, expert(): pl.pallas_call(functools.partial(expert_kernel, first, counts), in_specs=...  25.4 us
    unnamed x57, local copies, waits for them, and re-layouts  20.3 us
    ppermute x12, starting transfers between devices, shift(): lax.ppermute(x, 'etp', [(i, (i // 2 + by) % chips * 2 + i % 2) for i in r...  15.9 us
    pallas_call x6, Pallas kernels, add(): pl.pallas_call(functools.partial(add_kernel, tuple((start for _, start in...  10.3 us
    ppermute x3, waiting for transfers between devices, local(): lax.ppermute(column, 'etp', [(i, i ^ bit) for i in range(n_etp)])  9.98 us
  transfers between devices with their start and end apart: 31, of which 15 were waited for; matrix products, arithmetic and copies ran while one was open for 0% of the time, Pallas kernels for 19%

profile of v3, /device:TPU:6, one launch (start us, length us, event | category | flops | bytes accessed | tf_op | source)
XLA Modules:
  0.0 211.9 jit_solution(9970920851370407155)
XLA Ops:
  1.6 1.1 copy-done.15
  3.4 2.3 %pack_grad.1 = bf16[768,640]{1,0:T(8,128)(2,1)} custom-call(s32[1,128]{1,0:T(1,128)S(1)} %bitcast.40, bf16[128,2560]{1,0:T(8,128)(2,1)S(1)} %copy-done.15), custom_call_target="tpu_custom_call" | custom-call | bytes 1048576 | tf_op jit(solution)/shard_map/pack_grad/pallas_call | solution.py:66
  5.6 11.6 %all-to-all-start = ((bf16[32,24,640]{2,1,0:T(8,128)(2,1)}), bf16[32,24,640]{2,1,0:T(8,128)(2,1)}, u32[]{:S(2)}, u32[]{:S(2)}) async-start(bf16[32,24,640]{2,1,0:T(8,128)(2,1)} %bitcast.4), calls=%async_computation | async-start | bytes 1966080 | tf_op jit(solution)/shard_map/grads/all_to_all | solution.py:261
  17.3 1.3 pack_tok.1
  18.6 1.0 copy-done.7
  19.6 24.6 %all-to-all-done = bf16[32,24,640]{2,1,0:T(8,128)(2,1)} async-done(((bf16[32,24,640]{2,1,0:T(8,128)(2,1)}), bf16[32,24,640]{2,1,0:T(8,128)(2,1)}, u32[]{:S(2)}, u32[]{:S(2)}) %all-to-all-start) | async-done | bytes 983072 | tf_op jit(solution)/shard_map/grads/all_to_all | solution.py:261
  44.2 3.0 %unpack_grad.1 = (bf16[96,2560]{1,0:T(8,128)(2,1)}, bf16[96,2560]{1,0:T(8,128)(2,1)}) custom-call(bf16[768,640]{1,0:T(8,128)(2,1)} %bitcast.5.packed_ref), custom_call_target="tpu_custom_call" | custom-call | bytes 1048576 | tf_op jit(solution)/shard_map/unpack_grad/pallas_call | solution.py:89
  47.7 0.8 collective-permute-start.8
  48.5 2.4 %collective-permute-start.3 = (bf16[96,2560]{1,0:T(8,128)(2,1)}, bf16[96,2560]{1,0:T(8,128)(2,1)}, u32[]{:S(2)}, u32[]{:S(2)}) collective-permute-start(bf16[96,2560]{1,0:T(8,128)(2,1)} %get-tuple-element.39.refs_0_), channel_id=1, source_target_pairs={{0,2},{1,3},{2,4},{3,5},{4,6},{5,7},{6,0},{7,1},{8,10},{9,11},{10,... | collective-permute-start | bytes 1474568 | tf_op jit(solution)/shard_map/left0/ppermute | solution.py:291
  50.9 0.8 copy-done.18
  51.7 3.2 %collective-permute-start.4 = (bf16[96,2560]{1,0:T(8,128)(2,1)}, bf16[96,2560]{1,0:T(8,128)(2,1)}, u32[]{:S(2)}, u32[]{:S(2)}) collective-permute-start(bf16[96,2560]{1,0:T(8,128)(2,1)} %get-tuple-element.40.refs_1_), channel_id=1, source_target_pairs={{0,2},{1,3},{2,4},{3,5},{4,6},{5,7},{6,0},{7,1},{8,10},{9,11},{10,... | collective-permute-start | bytes 1474568 | tf_op jit(solution)/shard_map/left1/ppermute | solution.py:291
  55.0 5.4 %all-to-all-start.1 = ((bf16[32,24,640]{2,1,0:T(8,128)(2,1)}), bf16[32,24,640]{2,1,0:T(8,128)(2,1)}, u32[]{:S(2)}, u32[]{:S(2)}) async-start(bf16[32,24,640]{2,1,0:T(8,128)(2,1)} %bitcast.38), calls=%async_computation.1 | async-start | bytes 1966080 | tf_op jit(solution)/shard_map/toks/all_to_all | solution.py:261
  60.4 1.7 copy-done.2
  62.2 1.7 copy-done.3
  63.9 1.4 copy-done.4
  65.3 1.4 copy-done.6
  66.7 1.0 copy-done.19
  67.7 7.1 %expert_own.1 = (bf16[192,2560]{1,0:T(8,128)(2,1)S(1)}, bf16[192,2560]{1,0:T(8,128)(2,1)S(1)}) custom-call(s32[8]{0:T(128)S(1)} %reshape.41.ids_ref, bf16[96,2560]{1,0:T(8,128)(2,1)} %get-tuple-element.39.refs_0_, bf16[96,2560]{1,0:T(8,128)(2,1)} %get-tuple-element.40.refs_1_, bf16[96,2560]{1,0:T(8,128)(2,1)S(1)} %copy-done.19, ...), custom_call_target="tpu_custom_call" | custom-call | bytes 1048576 | tf_op jit(solution)/shard_map/expert_own/pallas_call | solution.py:156
  74.8 1.0 copy-done.13
  75.8 1.0 copy-done.22
  77.9 2.4 %collective-permute-done.9.refs_6_ = bf16[96,2560]{1,0:T(8,128)(2,1)S(1)} collective-permute-done((bf16[96,2560]{1,0:T(8,128)(2,1)}, bf16[96,2560]{1,0:T(8,128)(2,1)S(1)}, u32[]{:S(2)}, u32[]{:S(2)}) %collective-permute-start.9) | collective-permute-done | bytes 491552 | tf_op jit(solution)/shard_map/right_x0/ppermute | solution.py:295
  81.0 12.4 %expert_sides.1 = (bf16[192,2560]{1,0:T(8,128)(2,1)S(1)}, bf16[192,2560]{1,0:T(8,128)(2,1)S(1)}, bf16[192,2560]{1,0:T(8,128)(2,1)S(1)}, bf16[192,2560]{1,0:T(8,128)(2,1)S(1)}) custom-call(s32[8]{0:T(128)S(1)} %reshape.41.ids_ref, bf16[96,2560]{1,0:T(8,128)(2,1)} %collective-permute-done.3.refs_0_, bf16[96,2560]{1,0:T(8,128)(2,1)} %collective-permute-done.4.refs_1_, ...), custom_call_target="tpu_custom_call" | custom-call | bytes 1048576 | tf_op jit(solution)/shard_map/expert_sides/pallas_call | solution.py:156
  97.0 0.9 copy-done.8
  99.8 5.9 %expert_far.1 = (bf16[192,2560]{1,0:T(8,128)(2,1)S(1)}, bf16[192,2560]{1,0:T(8,128)(2,1)S(1)}) custom-call(s32[8]{0:T(128)S(1)} %reshape.41.ids_ref, bf16[96,2560]{1,0:T(8,128)(2,1)S(1)} %collective-permute-done.11.refs_0_, bf16[96,2560]{1,0:T(8,128)(2,1)S(1)} %collective-permute-done.14.refs_1_, bf16[96,2560]{1,0:T(8,128)(2,1)S(1)} %collective-permute-done.15.refs_2_, ...), custom_call_target="tpu_custom_call" | custom-call | bytes 1048576 | tf_op jit(solution)/shard_map/expert_far/pallas_call | solution.py:156
  105.8 1.0 copy-done.12
  106.8 1.0 copy-done.24
  107.9 3.2 %collective-permute-start.19 = (bf16[96,2560]{1,0:T(8,128)(2,1)}, bf16[96,2560]{1,0:T(8,128)(2,1)S(1)}, u32[]{:S(2)}, u32[]{:S(2)}) collective-permute-start(bf16[96,2560]{1,0:T(8,128)(2,1)} %copy-done.17), channel_id=1, source_target_pairs={{0,2},{1,3},{2,4},{3,5},{4,6},{5,7},{6,0},{7,1},{8,10},{9,11},{10,... | collective-permute-start | bytes 1474568 | tf_op jit(solution)/shard_map/to_right1/ppermute | solution.py:291
  111.1 1.0 copy-done.25
  112.1 2.1 sum_far0.1
  114.2 2.2 %collective-permute-start.20 = (bf16[96,2560]{1,0:T(8,128)(2,1)}, bf16[96,2560]{1,0:T(8,128)(2,1)S(1)}, u32[]{:S(2)}, u32[]{:S(2)}) collective-permute-start(bf16[96,2560]{1,0:T(8,128)(2,1)} %sum_far0.1), channel_id=1, source_target_pairs={{0,2},{1,3},{2,4},{3,5},{4,6},{5,7},{6,0},{7,1},{8,10},{9,11},{10,... | collective-permute-start | bytes 1474568 | tf_op jit(solution)/shard_map/via_right/ppermute | solution.py:291
  116.4 2.1 sum_far1.1
  118.7 2.1 %unpack_tok.1 = (bf16[96,2560]{1,0:T(8,128)(2,1)S(1)}, bf16[96,2560]{1,0:T(8,128)(2,1)S(1)}) custom-call(bf16[768,640]{1,0:T(8,128)(2,1)} %bitcast.12.packed_ref), custom_call_target="tpu_custom_call" | custom-call | bytes 1048576 | tf_op jit(solution)/shard_map/unpack_tok/pallas_call | solution.py:89
  120.8 1.8 collective-permute-done.18.refs_1_
  123.0 9.7 %collective-permute-done.20.refs_2_ = bf16[96,2560]{1,0:T(8,128)(2,1)S(1)} collective-permute-done((bf16[96,2560]{1,0:T(8,128)(2,1)}, bf16[96,2560]{1,0:T(8,128)(2,1)S(1)}, u32[]{:S(2)}, u32[]{:S(2)}) %collective-permute-start.20) | collective-permute-done | bytes 491552 | tf_op jit(solution)/shard_map/via_right/ppermute | solution.py:291
  133.5 2.3 %sum_right0.1 = bf16[96,2560]{1,0:T(8,128)(2,1)} custom-call(bf16[192,2560]{1,0:T(8,128)(2,1)} %copy-done.10, bf16[192,2560]{1,0:T(8,128)(2,1)} %copy-done.11, bf16[96,2560]{1,0:T(8,128)(2,1)} %copy-done.27), custom_call_target="tpu_custom_call" | custom-call | bytes 1048576 | tf_op jit(solution)/shard_map/sum_right0/pallas_call | solution.py:185
  135.8 3.7 %collective-permute-start.21 = (bf16[96,2560]{1,0:T(8,128)(2,1)}, bf16[96,2560]{1,0:T(8,128)(2,1)S(1)}, u32[]{:S(2)}, u32[]{:S(2)}) collective-permute-start(bf16[96,2560]{1,0:T(8,128)(2,1)} %sum_right0.1), channel_id=1, source_target_pairs={{0,2},{1,3},{2,4},{3,5},{4,6},{5,7},{6,0},{7,1},{8,10},{9,11},{10,... | collective-permute-start | bytes 1474568 | tf_op jit(solution)/shard_map/to_right0/ppermute | solution.py:291
  140.2 2.3 %sum_left1.1 = bf16[96,2560]{1,0:T(8,128)(2,1)} custom-call(bf16[192,2560]{1,0:T(8,128)(2,1)} %copy-done.8, bf16[192,2560]{1,0:T(8,128)(2,1)} %copy-done.9, bf16[96,2560]{1,0:T(8,128)(2,1)} %copy-done.26), custom_call_target="tpu_custom_call" | custom-call | bytes 1048576 | tf_op jit(solution)/shard_map/sum_left1/pallas_call | solution.py:185
  142.7 7.0 %collective-permute-done.21.refs_0_ = bf16[96,2560]{1,0:T(8,128)(2,1)S(1)} collective-permute-done((bf16[96,2560]{1,0:T(8,128)(2,1)}, bf16[96,2560]{1,0:T(8,128)(2,1)S(1)}, u32[]{:S(2)}, u32[]{:S(2)}) %collective-permute-start.21) | collective-permute-done | bytes 491552 | tf_op jit(solution)/shard_map/to_right0/ppermute | solution.py:291
  149.7 6.5 %collective-permute-done.23.refs_3_ = bf16[96,2560]{1,0:T(8,128)(2,1)S(1)} collective-permute-done((bf16[96,2560]{1,0:T(8,128)(2,1)}, bf16[96,2560]{1,0:T(8,128)(2,1)S(1)}, u32[]{:S(2)}, u32[]{:S(2)}) %collective-permute-start.23) | collective-permute-done | bytes 491552 | tf_op jit(solution)/shard_map/to_left1/ppermute | solution.py:291
  156.1 3.3 %token_math.1 = (bf16[768,640]{1,0:T(8,128)(2,1)}, f32[1,2560]{1,0:T(1,128)S(1)}) custom-call(bf16[1,2560]{1,0:T(2,128)(2,1)S(1)} %dynamic-slice_bitcast_fusion.router_ref, bf16[192,2560]{1,0:T(8,128)(2,1)S(1)} %copy-done.14, bf16[192,2560]{1,0:T(8,128)(2,1)S(1)} %collective-permute-done.2.keep_r_ref, bf16[96,2560]{1,0:T(8,128)(2,1)S(1)} %collective-permute-done.21.refs_0_, ...), custom_call_target="tpu_custom_call" | custom-call | bytes 1048576 | tf_op jit(solution)/shard_map/token_math/pallas_call | solution.py:227
  159.5 9.7 %all-to-all-start.2 = ((bf16[32,24,640]{2,1,0:T(8,128)(2,1)}), bf16[32,24,640]{2,1,0:T(8,128)(2,1)S(1)}, u32[]{:S(2)}, u32[]{:S(2)}) async-start(bf16[32,24,640]{2,1,0:T(8,128)(2,1)} %bitcast.13), calls=%async_computation.2 | async-start | bytes 1966080 | tf_op jit(solution)/shard_map/back/all_to_all | solution.py:261
  169.3 1.2 collective-permute-done.24
  170.6 3.7 %collective-permute-done.25 = f32[1,2560]{1,0:T(1,128)S(1)} collective-permute-done((f32[1,2560]{1,0:T(1,128)S(1)}, f32[1,2560]{1,0:T(1,128)S(1)}, u32[]{:S(2)}, u32[]{:S(2)}) %collective-permute-start.25) | collective-permute-done | bytes 10272 | tf_op jit(solution)/shard_map/ppermute | solution.py:339
  174.4 5.2 %collective-permute-done.26 = f32[1,2560]{1,0:T(1,128)S(1)} collective-permute-done((f32[1,2560]{1,0:T(1,128)S(1)}, f32[1,2560]{1,0:T(1,128)S(1)}, u32[]{:S(2)}, u32[]{:S(2)}) %collective-permute-start.26) | collective-permute-done | bytes 10272 | tf_op jit(solution)/shard_map/ppermute | solution.py:339
  179.5 15.1 %all-to-all-done.2 = bf16[32,24,640]{2,1,0:T(8,128)(2,1)S(1)} async-done(((bf16[32,24,640]{2,1,0:T(8,128)(2,1)}), bf16[32,24,640]{2,1,0:T(8,128)(2,1)S(1)}, u32[]{:S(2)}, u32[]{:S(2)}) %all-to-all-start.2) | async-done | bytes 983072 | tf_op jit(solution)/shard_map/back/all_to_all | solution.py:261
  195.4 5.0 %all-to-all-start.3 = ((bf16[32,4,640]{2,1,0:T(4,128)(2,1)}), bf16[32,4,640]{2,1,0:T(4,128)(2,1)S(1)}, u32[]{:S(2)}, u32[]{:S(2)}) async-start(bf16[32,4,640]{2,1,0:T(4,128)(2,1)} %broadcast_in_dim.8), calls=%async_computation.3 | async-start | bytes 327680 | tf_op jit(solution)/shard_map/all_to_all | solution.py:343
  200.4 1.8 final.1
  202.2 8.9 %all-to-all-done.3 = bf16[32,4,640]{2,1,0:T(4,128)(2,1)S(1)} async-done(((bf16[32,4,640]{2,1,0:T(4,128)(2,1)}), bf16[32,4,640]{2,1,0:T(4,128)(2,1)S(1)}, u32[]{:S(2)}, u32[]{:S(2)}) %all-to-all-start.3) | async-done | bytes 163872 | tf_op jit(solution)/shard_map/all_to_all | solution.py:343
  (98 shorter events, 13.6 us)
Async XLA Ops:
  0.6 16.6 %copy-start.21 = (s32[128,1]{0,1:T(1,128)S(1)}, s32[128,1]{0,1:T(1,128)}, u32[]{:S(2)}) copy-start(s32[128,1]{0,1:T(1,128)} %param.13) | copy-start | bytes 1540
  1.6 1.1 copy-start.15
  3.4 13.9 %copy-start.16 = (bf16[128,2560]{1,0:T(8,128)(2,1)S(1)}, bf16[128,2560]{1,0:T(8,128)(2,1)}, u32[]{:S(2)}) copy-start(bf16[128,2560]{1,0:T(8,128)(2,1)} %rows_ref.2) | copy-start | bytes 1966084
  5.6 38.5 %all-to-all-start = ((bf16[32,24,640]{2,1,0:T(8,128)(2,1)}), bf16[32,24,640]{2,1,0:T(8,128)(2,1)}, u32[]{:S(2)}, u32[]{:S(2)}) async-start(bf16[32,24,640]{2,1,0:T(8,128)(2,1)} %bitcast.4), calls=%async_computation | async-start | bytes 1966080 | tf_op jit(solution)/shard_map/grads/all_to_all | solution.py:261
  17.3 43.1 %copy-start.1 = (bf16[1,512,2560]{2,1,0:T(8,128)(2,1)S(1)}, bf16[1,512,2560]{2,1,0:T(8,128)(2,1)}, u32[]{:S(2)}) copy-start(bf16[1,512,2560]{2,1,0:T(8,128)(2,1)} %param.18) | copy-start | bytes 7864324
  47.2 3.8 %collective-permute-start = (bf16[96,2560]{1,0:T(8,128)(2,1)}, bf16[96,2560]{1,0:T(8,128)(2,1)S(1)}, u32[]{:S(2)}, u32[]{:S(2)}) collective-permute-start(bf16[96,2560]{1,0:T(8,128)(2,1)} %get-tuple-element.39.refs_0_), channel_id=1, source_target_pairs={{0,1},{1,0},{2,3},{3,2},{4,5},{5,4},{6,7},{7,6},{8,9},{9,8},{10,11... | collective-permute-start | bytes 1474568 | tf_op jit(solution)/shard_map/own_x0/ppermute | solution.py:295
  47.2 13.2 %collective-permute-start.1 = (bf16[96,2560]{1,0:T(8,128)(2,1)}, bf16[96,2560]{1,0:T(8,128)(2,1)}, u32[]{:S(2)}, u32[]{:S(2)}) collective-permute-start(bf16[96,2560]{1,0:T(8,128)(2,1)} %get-tuple-element.40.refs_1_), channel_id=1, source_target_pairs={{0,1},{1,0},{2,3},{3,2},{4,5},{5,4},{6,7},{7,6},{8,9},{9,8},{10,11... | collective-permute-start | bytes 1474568 | tf_op jit(solution)/shard_map/own_x1/ppermute | solution.py:295
  47.7 29.1 %collective-permute-start.8 = (bf16[96,2560]{1,0:T(8,128)(2,1)}, bf16[96,2560]{1,0:T(8,128)(2,1)S(1)}, u32[]{:S(2)}, u32[]{:S(2)}) collective-permute-start(bf16[96,2560]{1,0:T(8,128)(2,1)} %get-tuple-element.40.refs_1_), channel_id=1, source_target_pairs={{0,6},{1,7},{2,0},{3,1},{4,2},{5,3},{6,4},{7,5},{8,14},{9,15},{10,... | collective-permute-start | bytes 1474568 | tf_op jit(solution)/shard_map/right1/ppermute | solution.py:291
  48.5 28.3 %collective-permute-start.3 = (bf16[96,2560]{1,0:T(8,128)(2,1)}, bf16[96,2560]{1,0:T(8,128)(2,1)}, u32[]{:S(2)}, u32[]{:S(2)}) collective-permute-start(bf16[96,2560]{1,0:T(8,128)(2,1)} %get-tuple-element.39.refs_0_), channel_id=1, source_target_pairs={{0,2},{1,3},{2,4},{3,5},{4,6},{5,7},{6,0},{7,1},{8,10},{9,11},{10,... | collective-permute-start | bytes 1474568 | tf_op jit(solution)/shard_map/left0/ppermute | solution.py:291
  50.9 25.9 %collective-permute-start.7 = (bf16[96,2560]{1,0:T(8,128)(2,1)}, bf16[96,2560]{1,0:T(8,128)(2,1)}, u32[]{:S(2)}, u32[]{:S(2)}) collective-permute-start(bf16[96,2560]{1,0:T(8,128)(2,1)} %get-tuple-element.39.refs_0_), channel_id=1, source_target_pairs={{0,6},{1,7},{2,0},{3,1},{4,2},{5,3},{6,4},{7,5},{8,14},{9,15},{10,... | collective-permute-start | bytes 1474568 | tf_op jit(solution)/shard_map/right0/ppermute | solution.py:291
  51.7 25.6 %collective-permute-start.4 = (bf16[96,2560]{1,0:T(8,128)(2,1)}, bf16[96,2560]{1,0:T(8,128)(2,1)}, u32[]{:S(2)}, u32[]{:S(2)}) collective-permute-start(bf16[96,2560]{1,0:T(8,128)(2,1)} %get-tuple-element.40.refs_1_), channel_id=1, source_target_pairs={{0,2},{1,3},{2,4},{3,5},{4,6},{5,7},{6,0},{7,1},{8,10},{9,11},{10,... | collective-permute-start | bytes 1474568 | tf_op jit(solution)/shard_map/left1/ppermute | solution.py:291
  55.0 52.8 %all-to-all-start.1 = ((bf16[32,24,640]{2,1,0:T(8,128)(2,1)}), bf16[32,24,640]{2,1,0:T(8,128)(2,1)}, u32[]{:S(2)}, u32[]{:S(2)}) async-start(bf16[32,24,640]{2,1,0:T(8,128)(2,1)} %bitcast.38), calls=%async_computation.1 | async-start | bytes 1966080 | tf_op jit(solution)/shard_map/toks/all_to_all | solution.py:261
  60.4 1.7 copy-start.2
  62.2 1.7 copy-start.3
  63.9 1.4 copy-start.4
  65.3 1.4 copy-start.6
  66.7 1.0 copy-start.19
  67.7 13.3 %copy-start.5 = (bf16[1,1536,512]{2,1,0:T(8,128)(2,1)S(1)}, bf16[1,1536,512]{2,1,0:T(8,128)(2,1)}, u32[]{:S(2)}) copy-start(bf16[1,1536,512]{2,1,0:T(8,128)(2,1)} %param.14) | copy-start | bytes 4718596
  74.8 1.0 copy-start.13
  75.8 1.0 copy-start.22
  76.8 4.2 %collective-permute-start.5 = (bf16[96,2560]{1,0:T(8,128)(2,1)}, bf16[96,2560]{1,0:T(8,128)(2,1)S(1)}, u32[]{:S(2)}, u32[]{:S(2)}) collective-permute-start(bf16[96,2560]{1,0:T(8,128)(2,1)} %collective-permute-done.3.refs_0_), channel_id=1, source_target_pairs={{0,1},{1,0},{2,3},{3,2},{4,5},{5,4},{6,7},{7,6},{8,9},{9,8},{10,11... | collective-permute-start | bytes 1474568 | tf_op jit(solution)/shard_map/left_x0/ppermute | solution.py:295
  76.8 3.5 %collective-permute-start.9 = (bf16[96,2560]{1,0:T(8,128)(2,1)}, bf16[96,2560]{1,0:T(8,128)(2,1)S(1)}, u32[]{:S(2)}, u32[]{:S(2)}) collective-permute-start(bf16[96,2560]{1,0:T(8,128)(2,1)} %collective-permute-done.7.refs_4_), channel_id=1, source_target_pairs={{0,1},{1,0},{2,3},{3,2},{4,5},{5,4},{6,7},{7,6},{8,9},{9,8},{10,11... | collective-permute-start | bytes 1474568 | tf_op jit(solution)/shard_map/right_x0/ppermute | solution.py:295
  77.3 3.7 %collective-permute-start.6 = (bf16[96,2560]{1,0:T(8,128)(2,1)}, bf16[96,2560]{1,0:T(8,128)(2,1)S(1)}, u32[]{:S(2)}, u32[]{:S(2)}) collective-permute-start(bf16[96,2560]{1,0:T(8,128)(2,1)} %collective-permute-done.4.refs_1_), channel_id=1, source_target_pairs={{0,1},{1,0},{2,3},{3,2},{4,5},{5,4},{6,7},{7,6},{8,9},{9,8},{10,11... | collective-permute-start | bytes 1474568 | tf_op jit(solution)/shard_map/left_x1/ppermute | solution.py:295
  77.4 3.6 %collective-permute-start.10 = (bf16[96,2560]{1,0:T(8,128)(2,1)S(1)}, bf16[96,2560]{1,0:T(8,128)(2,1)S(1)}, u32[]{:S(2)}, u32[]{:S(2)}) collective-permute-start(bf16[96,2560]{1,0:T(8,128)(2,1)S(1)} %collective-permute-done.8.refs_5_), channel_id=1, source_target_pairs={{0,1},{1,0},{2,3},{3,2},{4,5},{5,4},{6,7},{7,6},{8,9},{9,8},{10,11... | collective-permute-start | bytes 1474568 | tf_op jit(solution)/shard_map/right_x1/ppermute | solution.py:295
  77.8 16.9 %collective-permute-start.11 = (bf16[96,2560]{1,0:T(8,128)(2,1)}, bf16[96,2560]{1,0:T(8,128)(2,1)S(1)}, u32[]{:S(2)}, u32[]{:S(2)}) collective-permute-start(bf16[96,2560]{1,0:T(8,128)(2,1)} %collective-permute-done.3.refs_0_), channel_id=1, source_target_pairs={{0,2},{1,3},{2,4},{3,5},{4,6},{5,7},{6,0},{7,1},{8,10},{9,11},{10,... | collective-permute-start | bytes 1474568 | tf_op jit(solution)/shard_map/far0/ppermute | solution.py:291
  80.3 14.5 %collective-permute-start.14 = (bf16[96,2560]{1,0:T(8,128)(2,1)S(1)}, bf16[96,2560]{1,0:T(8,128)(2,1)S(1)}, u32[]{:S(2)}, u32[]{:S(2)}) collective-permute-start(bf16[96,2560]{1,0:T(8,128)(2,1)S(1)} %collective-permute-done.8.refs_5_), channel_id=1, source_target_pairs={{0,6},{1,7},{2,0},{3,1},{4,2},{5,3},{6,4},{7,5},{8,14},{9,15},{10,... | collective-permute-start | bytes 1474568 | tf_op jit(solution)/shard_map/far1/ppermute | solution.py:291
  93.4 4.6 %copy-start.10 = (bf16[192,2560]{1,0:T(8,128)(2,1)}, bf16[192,2560]{1,0:T(8,128)(2,1)S(1)}, u32[]{:S(2)}) copy-start(bf16[192,2560]{1,0:T(8,128)(2,1)S(1)} %get-tuple-element.58.refs_0_) | copy-start | bytes 2949124
  93.4 2.7 %collective-permute-start.12 = (bf16[192,2560]{1,0:T(8,128)(2,1)S(1)}, bf16[192,2560]{1,0:T(8,128)(2,1)S(1)}, u32[]{:S(2)}, u32[]{:S(2)}) collective-permute-start(bf16[192,2560]{1,0:T(8,128)(2,1)S(1)} %get-tuple-element.49), channel_id=1, source_target_pairs={{0,1},{1,0},{2,3},{3,2},{4,5},{5,4},{6,7},{7,6},{8,9},{9,8},{10,11... | collective-permute-start | bytes 2949128 | tf_op jit(solution)/shard_map/left_sum/ppermute | solution.py:295
  93.6 4.3 %collective-permute-start.13 = (bf16[192,2560]{1,0:T(8,128)(2,1)S(1)}, bf16[192,2560]{1,0:T(8,128)(2,1)S(1)}, u32[]{:S(2)}, u32[]{:S(2)}) collective-permute-start(bf16[192,2560]{1,0:T(8,128)(2,1)S(1)} %get-tuple-element.50), channel_id=1, source_target_pairs={{0,1},{1,0},{2,3},{3,2},{4,5},{5,4},{6,7},{7,6},{8,9},{9,8},{10,11... | collective-permute-start | bytes 2949128 | tf_op jit(solution)/shard_map/right_sum/ppermute | solution.py:295
  94.8 5.0 %collective-permute-start.15 = (bf16[96,2560]{1,0:T(8,128)(2,1)S(1)}, bf16[96,2560]{1,0:T(8,128)(2,1)S(1)}, u32[]{:S(2)}, u32[]{:S(2)}) collective-permute-start(bf16[96,2560]{1,0:T(8,128)(2,1)S(1)} %collective-permute-done.11.refs_0_), channel_id=1, source_target_pairs={{0,1},{1,0},{2,3},{3,2},{4,5},{5,4},{6,7},{7,6},{8,9},{9,8},{10,11... | collective-permute-start | bytes 1474568 | tf_op jit(solution)/shard_map/far_x0/ppermute | solution.py:295
  94.8 5.0 %collective-permute-start.16 = (bf16[96,2560]{1,0:T(8,128)(2,1)S(1)}, bf16[96,2560]{1,0:T(8,128)(2,1)S(1)}, u32[]{:S(2)}, u32[]{:S(2)}) collective-permute-start(bf16[96,2560]{1,0:T(8,128)(2,1)S(1)} %collective-permute-done.14.refs_1_), channel_id=1, source_target_pairs={{0,1},{1,0},{2,3},{3,2},{4,5},{5,4},{6,7},{7,6},{8,9},{9,8},{10,11... | collective-permute-start | bytes 1474568 | tf_op jit(solution)/shard_map/far_x1/ppermute | solution.py:295
  98.0 1.0 copy-start.11
  105.8 1.0 copy-start.12
  107.7 10.9 %copy-start.23 = (bf16[192,2560]{1,0:T(8,128)(2,1)S(1)}, bf16[192,2560]{1,0:T(8,128)(2,1)}, u32[]{:S(2)}) copy-start(bf16[192,2560]{1,0:T(8,128)(2,1)} %copy-done.22) | copy-start | bytes 2949124
  107.7 3.4 %collective-permute-start.17 = (bf16[192,2560]{1,0:T(8,128)(2,1)}, bf16[192,2560]{1,0:T(8,128)(2,1)S(1)}, u32[]{:S(2)}, u32[]{:S(2)}) collective-permute-start(bf16[192,2560]{1,0:T(8,128)(2,1)} %copy-done.24), channel_id=1, source_target_pairs={{0,1},{1,0},{2,3},{3,2},{4,5},{5,4},{6,7},{7,6},{8,9},{9,8},{10,11... | collective-permute-start | bytes 2949128 | tf_op jit(solution)/shard_map/far_sum/ppermute | solution.py:295
  107.9 14.8 %collective-permute-start.18 = (bf16[96,2560]{1,0:T(8,128)(2,1)S(1)}, bf16[96,2560]{1,0:T(8,128)(2,1)S(1)}, u32[]{:S(2)}, u32[]{:S(2)}) collective-permute-start(bf16[96,2560]{1,0:T(8,128)(2,1)S(1)} %sum_left0.1), channel_id=1, source_target_pairs={{0,6},{1,7},{2,0},{3,1},{4,2},{5,3},{6,4},{7,5},{8,14},{9,15},{10,... | collective-permute-start | bytes 1474568 | tf_op jit(solution)/shard_map/to_left0/ppermute | solution.py:291
  107.9 15.2 %collective-permute-start.19 = (bf16[96,2560]{1,0:T(8,128)(2,1)}, bf16[96,2560]{1,0:T(8,128)(2,1)S(1)}, u32[]{:S(2)}, u32[]{:S(2)}) collective-permute-start(bf16[96,2560]{1,0:T(8,128)(2,1)} %copy-done.17), channel_id=1, source_target_pairs={{0,2},{1,3},{2,4},{3,5},{4,6},{5,7},{6,0},{7,1},{8,10},{9,11},{10,... | collective-permute-start | bytes 1474568 | tf_op jit(solution)/shard_map/to_right1/ppermute | solution.py:291
  114.2 18.5 %collective-permute-start.20 = (bf16[96,2560]{1,0:T(8,128)(2,1)}, bf16[96,2560]{1,0:T(8,128)(2,1)S(1)}, u32[]{:S(2)}, u32[]{:S(2)}) collective-permute-start(bf16[96,2560]{1,0:T(8,128)(2,1)} %sum_far0.1), channel_id=1, source_target_pairs={{0,2},{1,3},{2,4},{3,5},{4,6},{5,7},{6,0},{7,1},{8,10},{9,11},{10,... | collective-permute-start | bytes 1474568 | tf_op jit(solution)/shard_map/via_right/ppermute | solution.py:291
  118.5 21.0 %collective-permute-start.22 = (bf16[96,2560]{1,0:T(8,128)(2,1)}, bf16[96,2560]{1,0:T(8,128)(2,1)S(1)}, u32[]{:S(2)}, u32[]{:S(2)}) collective-permute-start(bf16[96,2560]{1,0:T(8,128)(2,1)} %sum_far1.1), channel_id=1, source_target_pairs={{0,6},{1,7},{2,0},{3,1},{4,2},{5,3},{6,4},{7,5},{8,14},{9,15},{10,... | collective-permute-start | bytes 1474568 | tf_op jit(solution)/shard_map/via_left/ppermute | solution.py:291
  118.7 24.0 %collective-permute-start.2 = (bf16[192,2560]{1,0:T(8,128)(2,1)S(1)}, bf16[192,2560]{1,0:T(8,128)(2,1)S(1)}, u32[]{:S(2)}, u32[]{:S(2)}) collective-permute-start(bf16[192,2560]{1,0:T(8,128)(2,1)S(1)} %copy-done.23), channel_id=1, source_target_pairs={{0,1},{1,0},{2,3},{3,2},{4,5},{5,4},{6,7},{7,6},{8,9},{9,8},{10,11... | collective-permute-start | bytes 2949128 | tf_op jit(solution)/shard_map/own_sum/ppermute | solution.py:295
  123.0 33.1 %copy-start.14 = (bf16[192,2560]{1,0:T(8,128)(2,1)S(1)}, bf16[192,2560]{1,0:T(8,128)(2,1)}, u32[]{:S(2)}) copy-start(bf16[192,2560]{1,0:T(8,128)(2,1)} %copy-done.13) | copy-start | bytes 2949124
  135.8 13.9 %collective-permute-start.21 = (bf16[96,2560]{1,0:T(8,128)(2,1)}, bf16[96,2560]{1,0:T(8,128)(2,1)S(1)}, u32[]{:S(2)}, u32[]{:S(2)}) collective-permute-start(bf16[96,2560]{1,0:T(8,128)(2,1)} %sum_right0.1), channel_id=1, source_target_pairs={{0,2},{1,3},{2,4},{3,5},{4,6},{5,7},{6,0},{7,1},{8,10},{9,11},{10,... | collective-permute-start | bytes 1474568 | tf_op jit(solution)/shard_map/to_right0/ppermute | solution.py:291
  142.6 13.6 %collective-permute-start.23 = (bf16[96,2560]{1,0:T(8,128)(2,1)}, bf16[96,2560]{1,0:T(8,128)(2,1)S(1)}, u32[]{:S(2)}, u32[]{:S(2)}) collective-permute-start(bf16[96,2560]{1,0:T(8,128)(2,1)} %sum_left1.1), channel_id=1, source_target_pairs={{0,6},{1,7},{2,0},{3,1},{4,2},{5,3},{6,4},{7,5},{8,14},{9,15},{10,... | collective-permute-start | bytes 1474568 | tf_op jit(solution)/shard_map/to_left1/ppermute | solution.py:291
  159.5 35.2 %all-to-all-start.2 = ((bf16[32,24,640]{2,1,0:T(8,128)(2,1)}), bf16[32,24,640]{2,1,0:T(8,128)(2,1)S(1)}, u32[]{:S(2)}, u32[]{:S(2)}) async-start(bf16[32,24,640]{2,1,0:T(8,128)(2,1)} %bitcast.13), calls=%async_computation.2 | async-start | bytes 1966080 | tf_op jit(solution)/shard_map/back/all_to_all | solution.py:261
  169.2 1.3 collective-permute-start.24
  170.5 3.8 %collective-permute-start.25 = (f32[1,2560]{1,0:T(1,128)S(1)}, f32[1,2560]{1,0:T(1,128)S(1)}, u32[]{:S(2)}, u32[]{:S(2)}) collective-permute-start(f32[1,2560]{1,0:T(1,128)S(1)} %add.47), channel_id=1, source_target_pairs={{0,2},{1,3},{2,0},{3,1},{4,6},{5,7},{6,4},{7,5},{8,10},{9,11},{10,... | collective-permute-start | bytes 30728 | tf_op jit(solution)/shard_map/ppermute | solution.py:339
  174.3 5.3 %collective-permute-start.26 = (f32[1,2560]{1,0:T(1,128)S(1)}, f32[1,2560]{1,0:T(1,128)S(1)}, u32[]{:S(2)}, u32[]{:S(2)}) collective-permute-start(f32[1,2560]{1,0:T(1,128)S(1)} %add.48), channel_id=1, source_target_pairs={{0,4},{1,5},{2,6},{3,7},{4,0},{5,1},{6,2},{7,3},{8,12},{9,13},{10,... | collective-permute-start | bytes 30728 | tf_op jit(solution)/shard_map/ppermute | solution.py:339
  195.4 15.7 %all-to-all-start.3 = ((bf16[32,4,640]{2,1,0:T(4,128)(2,1)}), bf16[32,4,640]{2,1,0:T(4,128)(2,1)S(1)}, u32[]{:S(2)}, u32[]{:S(2)}) async-start(bf16[32,4,640]{2,1,0:T(4,128)(2,1)} %broadcast_in_dim.8), calls=%async_computation.3 | async-start | bytes 327680 | tf_op jit(solution)/shard_map/all_to_all | solution.py:343
  (11 other events, 9.6 us)
